TPU v7x, 32 devices: a whole 2x2x4 slice. The times are simulated.
32 devices in a mesh: dp: 16 (over z, y, x), tensor: 2 (over core).
Axes of the slice: x: 2, y: 2, z: 4, core: 2. Of those that a mesh axis runs over, the one named last changes fastest.
Arguments:
- tokens: bfloat16 [32768, 768], P('dp'), may hold values from -6 to 6
- first_values: bfloat16 [32768, 384], P('dp'), may hold values from -6 to 6
- seq_count: int32 [16], P('dp'), may hold values from 1 to 2, as said below
- skip_map: int32 [6], P('tensor'), may hold values from 0 to 5, as said below
- norm1_gain: float32 [768], replicated, may hold values from 0.5 to 1.5
- norm1_shift: float32 [768], replicated, may hold values from -1 to 1
- query_weight: bfloat16 [768, 768], P(None, 'tensor'), may hold values from -0.3125 to 0.3125
- key_weight: bfloat16 [768, 768], P(None, 'tensor'), may hold values from -0.3125 to 0.3125
- value_weight: bfloat16 [768, 384], P(None, 'tensor'), may hold values from -0.21875 to 0.21875
- out_weight: bfloat16 [768, 768], P('tensor'), may hold values from -1.75 to 1.75
- norm2_gain: float32 [768], replicated, may hold values from 0.5 to 1.5
- norm2_shift: float32 [768], replicated, may hold values from -1 to 1
- up_weight: bfloat16 [768, 3072], P(None, 'tensor'), may hold values from -0.21875 to 0.21875
- down_weight: bfloat16 [3072, 768], P('tensor'), may hold values from -0.109375 to 0.109375
- cotangent: bfloat16 [32768, 768], P('dp'), may hold values from -6 to 6
Outputs:
- layer_out: float32 [32768, 768], P('dp')
- input_grad: float32 [32768, 768], P('dp')
- first_value_grad: float32 [32768, 384], P('dp', 'tensor')
- norm1_gain_grad: float32 [768], P('dp')
- norm1_shift_grad: float32 [768], P('dp')
- query_weight_grad: float32 [768, 768], P('dp', 'tensor')
- key_weight_grad: float32 [768, 768], P('dp', 'tensor')
- value_weight_grad: float32 [768, 384], P('dp', 'tensor')
- out_weight_grad: float32 [768, 768], P('tensor', 'dp')
- norm2_gain_grad: float32 [768], P('dp')
- norm2_shift_grad: float32 [768], P('dp')
- up_weight_grad: float32 [768, 3072], P('dp', 'tensor')
- down_weight_grad: float32 [3072, 768], P('tensor', 'dp')
Inputs may be any that keep to these rules, and one draw needn't show every extreme that they name: `seq_count`: some index of dp holds 2 live sequences in every draw; slots below the count are live. `skip_map`: A permutation: each first-layer value head is read by exactly one slot; the slots of each index of tensor read exactly one head of the other index's half.
All inputs are finite; a program needn't handle non-finite values.
Results may differ from a plain program's by a relative error of at most 0.012.
The roundings to bfloat16 on the way count: a program that leaves them out, or rounds other values in their place, can miss the bound.
Values sent between devices are 32-bit elements; how exact they have to be, the bound alone decides.
A program may use at most 192 MiB of HBM per device.

v0:
```python
import functools

import jax
import jax.numpy as jnp
from jax import lax
from jax.experimental import pallas as pl
from jax.experimental.pallas import tpu as pltpu
from jax.sharding import PartitionSpec as P

HEAD_DIM = 64
SEQ_LEN = 1024
BLOCK = 256
PAIR = 2 * HEAD_DIM
EPS = 1e-05
FILL = -1e30
VMEM_BYTES = 60 * 1024 * 1024

F32 = jnp.float32
BF16 = jnp.bfloat16


def dot_nn(left, right):
    return lax.dot_general(left, right, (((1,), (0,)), ((), ())), preferred_element_type=F32)


def dot_nt(left, right):
    return lax.dot_general(left, right, (((1,), (1,)), ((), ())), preferred_element_type=F32)


def norm_stats(values_in):
    average = jnp.mean(values_in, axis=-1, keepdims=True)
    centered = values_in - average
    variance = jnp.mean(centered * centered, axis=-1, keepdims=True)
    factor = lax.rsqrt(variance + EPS)
    return centered * factor, factor


def norm_backward(grad, normed, factor, gain):
    scaled = grad * gain
    mean_plain = jnp.mean(scaled, axis=-1, keepdims=True)
    mean_cross = jnp.mean(scaled * normed, axis=-1, keepdims=True)
    return factor * (scaled - mean_plain - normed * mean_cross)


def each(count, body):
    lax.fori_loop(0, count, lambda index, carry: (body(index), carry)[1], 0)


def row_block(index):
    return pl.ds(pl.multiple_of(index * BLOCK, BLOCK), BLOCK)


def recast(source, target, rows=64):
    def one(index):
        part = pl.ds(pl.multiple_of(index * rows, rows), rows)
        target[part, :] = source[part, :].astype(target.dtype)

    each(source.shape[0] // rows, one)


def head_masks(rows):
    lanes = lax.broadcasted_iota(jnp.int32, (rows, PAIR), 1)
    return lanes < HEAD_DIM


def split_heads(pair_rows):
    first = head_masks(pair_rows.shape[0])
    zero = jnp.zeros_like(pair_rows)
    return jnp.where(first, pair_rows, zero), jnp.where(first, zero, pair_rows)


MESH = pl.DeviceIdType.MESH


def params(collective_id):
    return pltpu.CompilerParams(
        vmem_limit_bytes=VMEM_BYTES, collective_id=collective_id, has_side_effects=True
    )


def fixed(shape):
    zeros = (0,) * len(shape)
    return pl.BlockSpec(shape, lambda i: zeros, pipeline_mode=pl.Buffered(1))


ANY = pl.BlockSpec(memory_space=pl.ANY)
SMEM = pl.BlockSpec(memory_space=pltpu.SMEM)


def ring_of(dp_size, width):
    rows = width // dp_size
    return dp_size % 8 == 0 and width % dp_size == 0 and rows % 8 == 0


def place(ring, width, dp_size, columns):
    if not ring:
        return (width, columns)
    return (dp_size // 4, 2, 2, width // dp_size, columns)


class Link:
    def __init__(self, dp_size):
        self.dp = lax.axis_index("dp")
        self.core = lax.axis_index("tensor")
        self.depth = dp_size // 4
        self.x = lax.rem(self.dp, 2)
        self.y = lax.rem(lax.div(self.dp, 2), 2)
        self.z = lax.div(self.dp, 4)
        self.peer = {"tensor": 1 - self.core}
        self.x_side = {"dp": self.dp + 1 - 2 * self.x}
        self.y_side = {"dp": self.dp + 2 - 4 * self.y}

    def z_place(self, hop):
        return lax.rem(self.z + hop, self.depth)

    def z_side(self, hop):
        return {"dp": 4 * self.z_place(hop) + lax.rem(self.dp, 4)}

    def meet(self, partners):
        barrier = pltpu.get_barrier_semaphore()
        for partner in partners:
            pl.semaphore_signal(barrier, inc=1, device_id=partner, device_id_type=MESH)
        pl.semaphore_wait(barrier, len(partners))


def remote(source, target, sems, index, device):
    send, recv = sems
    return pltpu.make_async_remote_copy(
        src_ref=source,
        dst_ref=target,
        send_sem=send.at[index],
        recv_sem=recv.at[index],
        device_id=device,
        device_id_type=MESH,
    )


def first_hop(link, source, landing, sems, base):
    low = link.depth // 2
    return [
        remote(
            source.at[0:low, :, 1 - link.x], landing.at[0], sems, base, link.x_side
        ),
        remote(
            source.at[low : 2 * low, 1 - link.y],
            landing.at[1],
            sems,
            base + 1,
            link.y_side,
        ),
    ]


def second_hop(link, source, landing, sems, base):
    low = link.depth // 2
    return [
        remote(
            source.at[0, :, 1 - link.y],
            landing.at[0:low],
            sems,
            base,
            link.y_side,
        ),
        remote(
            source.at[1, :, 1 - link.x],
            landing.at[low : 2 * low],
            sems,
            base + 1,
            link.x_side,
        ),
    ]


def last_hop(link, source, landing, sems, base):
    return [
        remote(
            source.at[link.z_place(hop)],
            landing.at[hop - 1],
            sems,
            base + hop - 1,
            link.z_side(hop),
        )
        for hop in range(1, link.depth)
    ]


def go(copies):
    for copy in copies:
        copy.start()


def finish(copies):
    for copy in copies:
        copy.wait()


def merge_first(link, whole, landing):
    low = link.depth // 2

    def one(row):
        for other in range(2):
            landing[0, row, other] += whole[row, other, link.x]
            landing[1, row, other] += whole[low + row, link.y, other]

    each(low, one)


def merge_second(link, landed, landing):
    low = link.depth // 2

    def one(row):
        landing[row] += landed[0, row, link.y]
        landing[low + row] += landed[1, row, link.x]

    each(low, one)


def total_last(own, landing):
    total = own
    for hop in range(landing.shape[0]):
        total = total + landing[hop]
    return total


HOPS = 7


class Chunk:
    def __init__(self, link, sems, base, whole=None, hop1=None, hop2=None, hop3=None):
        self.link, self.whole, self.hop1, self.hop2, self.hop3 = link, whole, hop1, hop2, hop3
        self.sems, self.base = sems, base
        self.sources = [whole, hop1, hop2]

    def hop(self, number):
        source = self.sources[number - 1]
        if number == 1:
            return first_hop(self.link, source, self.hop1, self.sems, self.base)
        if number == 2:
            return second_hop(self.link, source, self.hop2, self.sems, self.base + 2)
        return last_hop(self.link, source, self.hop3, self.sems, self.base + 4)

    def start(self, number):
        go(self.hop(number))

    def land(self, number):
        finish(self.hop(number))
        if number == 1:
            merge_first(self.link, self.whole, self.hop1)
        elif number == 2:
            merge_second(self.link, self.hop1, self.hop2)

    def total(self):
        finish(self.hop(3))
        return total_last(self.hop2[self.link.z], self.hop3)


class DeepChunk:
    def __init__(self, link, sems, base, whole, hop1, summed, source, hop2, hop3):
        self.link, self.whole, self.hop1, self.hop2, self.hop3 = link, whole, hop1, hop2, hop3
        self.summed, self.source = summed, source
        self.sems, self.base = sems, base

    def hop(self, number):
        link, sems, base = self.link, self.sems, self.base
        if number == 1:
            return last_hop(link, self.whole, self.hop1, sems, base)
        side = self.hop3.shape[-1]
        left, right = pl.ds(0, side), pl.ds(side, side)
        if number == 2:
            base += link.depth - 1
            summed = self.source
            return [
                remote(
                    summed.at[:, 1 - link.x, :, left], self.hop2.at[0], sems, base, link.x_side
                ),
                remote(
                    summed.at[1 - link.y, :, :, right], self.hop2.at[1], sems, base + 1, link.y_side
                ),
            ]
        base += link.depth + 1
        return [
            remote(self.hop2.at[0, 1 - link.y], self.hop3.at[0], sems, base, link.y_side),
            remote(self.hop2.at[1, 1 - link.x], self.hop3.at[1], sems, base + 1, link.x_side),
        ]

    def start(self, number):
        go(self.hop(number))

    def land(self, number):
        link = self.link
        finish(self.hop(number))
        if number == 1:

            def one(row):
                for other in range(2):
                    total = self.whole[link.z, row, other]
                    for hop in range(self.hop1.shape[0]):
                        total = total + self.hop1[hop, row, other]
                    self.summed[row, other] = total

            each(2, one)
        else:
            side = self.hop3.shape[-1]
            for other in range(2):
                self.hop2[0, other] += self.summed[other, link.x, :, 0:side]
                self.hop2[1, other] += self.summed[link.y, other, :, side:]

    def total(self):
        finish(self.hop(3))
        return jnp.concatenate(
            [self.hop2[0, self.link.y] + self.hop3[0], self.hop2[1, self.link.x] + self.hop3[1]],
            axis=-1,
        )


def front_kernel(
    dp_size,
    tokens,
    first_values,
    skip_map,
    gain_ref,
    shift_ref,
    wq_ref,
    wk_ref,
    wv_ref,
    out_w,
    up_w,
    down_w,
    n1_ref,
    q_ref,
    k_ref,
    v_ref,
    att_ref,
    lse_ref,
    w_ref,
    sel_ref,
    out_peer,
    up_peer,
    down_peer,
    x_scr,
    fv_scr,
    proj_own,
    proj_send,
    proj_recv,
    sel_send,
    sel_recv,
    out_low,
    up_low,
    down_low,
    out_send,
    up_send,
    down_send,
    out_recv,
    up_recv,
    down_recv,
    lse_scr,
    local_sem,
    send_sem,
    recv_sem,
):
    step = pl.program_id(0)
    length, width = x_scr.shape
    blocks = length // BLOCK
    half = pl.num_programs(0) // 2
    own_width = wq_ref.shape[1]
    fresh_width = wv_ref.shape[0]
    fv_width = fv_scr.shape[1]
    link = Link(dp_size)
    sems = (send_sem, recv_sem)
    rows_here = pl.ds(link.core * length, length)
    local = [
        pltpu.make_async_copy(tokens.at[rows_here], x_scr, local_sem.at[0]),
        pltpu.make_async_copy(first_values.at[rows_here], fv_scr, local_sem.at[1]),
        pltpu.make_async_copy(up_w, up_low, local_sem.at[2]),
        pltpu.make_async_copy(down_w, down_low, local_sem.at[3]),
        pltpu.make_async_copy(out_w, out_low, local_sem.at[4]),
    ]
    early = [
        remote(proj_send, proj_recv, sems, 0, link.peer),
        remote(sel_send, sel_recv, sems, 1, link.peer),
    ]
    late = [
        remote(up_send, up_recv, sems, 2, link.peer),
        remote(down_send, down_recv, sems, 3, link.peer),
        remote(out_send, out_recv, sems, 4, link.peer),
    ]
    landed = [
        (late[0], up_recv, up_low, pltpu.make_async_copy(up_low, up_peer, local_sem.at[2])),
        (late[1], down_recv, down_low, pltpu.make_async_copy(down_low, down_peer, local_sem.at[3])),
        (late[2], out_recv, out_low, pltpu.make_async_copy(out_low, out_peer, local_sem.at[4])),
    ]

    @pl.when(step == 0)
    def _():
        go(local)
        proj_own[2, :, 0:fresh_width] = jnp.transpose(wv_ref[...])
        proj_own[2, :, fresh_width:] = jnp.zeros((width, own_width - fresh_width), BF16)
        for part, source in enumerate((wq_ref, wk_ref)):
            recast(source, proj_own.at[part])
        for part in range(3):
            recast(proj_own.at[part], proj_send.at[part])
        row = lax.broadcasted_iota(jnp.int32, (fv_width, own_width), 0)
        col = lax.broadcasted_iota(jnp.int32, (fv_width, own_width), 1)
        slots = (own_width - fresh_width) // HEAD_DIM
        target = jnp.full((fv_width, own_width), -1, jnp.int32)
        for slot in range(slots):
            start = fresh_width + slot * HEAD_DIM
            inside = jnp.logical_and(col >= start, col < start + HEAD_DIM)
            target = jnp.where(inside, skip_map[slot] * HEAD_DIM + col - start, target)
        chosen = jnp.where(row == target, 1.0, 0.0).astype(F32)
        sel_send[...] = chosen
        sel_ref[:, 0:own_width] = chosen.astype(BF16)
        link.meet([link.peer])
        go(early)
        lse_scr[...] = jnp.zeros_like(lse_scr)
        local[0].wait()
        local[1].wait()

        def one(block, carry):
            rows = pl.ds(block * BLOCK, BLOCK)
            normed, _ = norm_stats(x_scr[rows, :].astype(F32))
            n1_ref[rows, :] = (normed * gain_ref[...] + shift_ref[...]).astype(BF16)
            return carry

        lax.fori_loop(0, blocks, one, 0)

    @pl.when(step == half)
    def _():
        finish(early)
        sel_ref[:, own_width:] = sel_recv[...].astype(BF16)

    @pl.when(step < half)
    def _():
        cols = pl.ds(pl.multiple_of(step * PAIR, PAIR), PAIR)
        for part in range(3):
            w_ref[:, part * PAIR : (part + 1) * PAIR] = proj_own[part, :, cols]

    @pl.when(step >= half)
    def _():
        cols = pl.ds(pl.multiple_of((step - half) * PAIR, PAIR), PAIR)
        for part in range(3):
            w_ref[:, part * PAIR : (part + 1) * PAIR] = proj_recv[part, :, cols].astype(BF16)

    sel_cols = pl.ds(pl.multiple_of(step * PAIR, PAIR), PAIR)
    for block in range(blocks):
        rows = slice(block * BLOCK, (block + 1) * BLOCK)
        fused = dot_nn(n1_ref[rows, :], w_ref[...])
        picked = dot_nn(fv_scr[rows, :], sel_ref[:, sel_cols])
        q_ref[rows, :] = (fused[:, 0:PAIR].astype(BF16).astype(F32) * HEAD_DIM**-0.5).astype(BF16)
        k_ref[rows, :] = fused[:, PAIR : 2 * PAIR].astype(BF16)
        v_ref[rows, :] = (fused[:, 2 * PAIR :] + picked).astype(BF16)

    lane = lax.broadcasted_iota(jnp.int32, (BLOCK, PAIR), 1)
    row_pos = lax.broadcasted_iota(jnp.int32, (BLOCK, BLOCK), 0)
    col_pos = lax.broadcasted_iota(jnp.int32, (BLOCK, BLOCK), 1)
    seen = col_pos <= row_pos
    for block in range(blocks):
        lo, hi = block * BLOCK, (block + 1) * BLOCK
        queries = split_heads(q_ref[lo:hi, :])
        total = jnp.zeros((BLOCK, PAIR), F32)
        lse_tile = lse_scr[lo:hi, :]
        for head in range(2):
            diag = jnp.where(seen, dot_nt(queries[head], k_ref[lo:hi, :]), FILL)
            peak = jnp.max(diag, axis=-1, keepdims=True)
            if block:
                past = dot_nt(queries[head], k_ref[0:lo, :])
                peak = jnp.maximum(peak, jnp.max(past, axis=-1, keepdims=True))
            diag = jnp.exp(diag - peak)
            mass = jnp.sum(diag, axis=-1, keepdims=True)
            if block:
                past = jnp.exp(past - peak)
                mass = mass + jnp.sum(past, axis=-1, keepdims=True)
            inverse = 1.0 / mass
            total = total + dot_nn((diag * inverse).astype(BF16), split_heads(v_ref[lo:hi, :])[head])
            if block:
                total = total + dot_nn(
                    (past * inverse).astype(BF16), split_heads(v_ref[0:lo, :])[head]
                )
            lse_tile = jnp.where(lane == 2 * step + head, peak + jnp.log(mass), lse_tile)
        att_ref[lo:hi, :] = total.astype(BF16)
        lse_scr[lo:hi, :] = lse_tile

    @pl.when(step == 0)
    def _():
        for copy in local[2:]:
            copy.wait()
        recast(up_low, up_send)
        recast(down_low, down_send)
        recast(out_low, out_send)
        go(late)

    @pl.when(step == pl.num_programs(0) - 2)
    def _():
        for copy, recv, low, store in landed:
            copy.wait()
            recast(recv, low)
            store.start()

    @pl.when(step == pl.num_programs(0) - 1)
    def _():
        for block in range(blocks):
            lo, hi = block * BLOCK, (block + 1) * BLOCK
            turned = jnp.transpose(lse_scr[lo:hi, :])
            for pair in range(lse_ref.shape[0]):
                lse_ref[pair, 0:2, lo:hi] = turned[2 * pair : 2 * pair + 2, :]
        for _, _, _, store in landed:
            store.wait()


def front(dp_size, tokens, first_values, skip_map, gain, shift, wq, wk, wv, out_w, up_w, down_w):
    width = tokens.shape[1]
    own_width = wq.shape[1]
    half = own_width // PAIR
    fv_width = first_values.shape[1]
    pair_block = pl.BlockSpec((SEQ_LEN, PAIR), lambda i: (0, i))
    pair_out = jax.ShapeDtypeStruct((SEQ_LEN, 2 * own_width), BF16)
    return pl.pallas_call(
        functools.partial(front_kernel, dp_size),
        grid=(2 * half,),
        in_specs=[
            ANY,
            ANY,
            SMEM,
            fixed((1, width)),
            fixed((1, width)),
            fixed(wq.shape),
            fixed(wk.shape),
            fixed(wv.shape),
            ANY,
            ANY,
            ANY,
        ],
        out_specs=[
            fixed((SEQ_LEN, width)),
            pair_block,
            pair_block,
            pair_block,
            pair_block,
            fixed((2 * half, 8, SEQ_LEN)),
            pl.BlockSpec((width, 3 * PAIR), lambda i: (0, i)),
            fixed((fv_width, 2 * own_width)),
            ANY,
            ANY,
            ANY,
        ],
        scratch_shapes=[
            pltpu.VMEM((SEQ_LEN, width), BF16),
            pltpu.VMEM((SEQ_LEN, fv_width), BF16),
            pltpu.VMEM((3, width, own_width), BF16),
            pltpu.VMEM((3, width, own_width), F32),
            pltpu.VMEM((3, width, own_width), F32),
            pltpu.VMEM((fv_width, own_width), F32),
            pltpu.VMEM((fv_width, own_width), F32),
            pltpu.VMEM(out_w.shape, BF16),
            pltpu.VMEM(up_w.shape, BF16),
            pltpu.VMEM(down_w.shape, BF16),
            pltpu.VMEM(out_w.shape, F32),
            pltpu.VMEM(up_w.shape, F32),
            pltpu.VMEM(down_w.shape, F32),
            pltpu.VMEM(out_w.shape, F32),
            pltpu.VMEM(up_w.shape, F32),
            pltpu.VMEM(down_w.shape, F32),
            pltpu.VMEM((SEQ_LEN, PAIR), F32),
            pltpu.SemaphoreType.DMA((5,)),
            pltpu.SemaphoreType.DMA((5,)),
            pltpu.SemaphoreType.DMA((5,)),
        ],
        out_shape=[
            jax.ShapeDtypeStruct((SEQ_LEN, width), BF16),
            pair_out,
            pair_out,
            pair_out,
            pair_out,
            jax.ShapeDtypeStruct((2 * half, 8, SEQ_LEN), F32),
            jax.ShapeDtypeStruct((width, 6 * own_width), BF16),
            jax.ShapeDtypeStruct((fv_width, 2 * own_width), BF16),
            jax.ShapeDtypeStruct(out_w.shape, BF16),
            jax.ShapeDtypeStruct(up_w.shape, BF16),
            jax.ShapeDtypeStruct(down_w.shape, BF16),
        ],
        compiler_params=params(0),
        name="front",
    )(tokens, first_values, skip_map, gain, shift, wq, wk, wv, out_w, up_w, down_w)


def gelu_pair(upper):
    scale = (2.0 / jnp.pi) ** 0.5
    square = upper * upper
    inner = upper * (scale + (scale * 0.044715) * square)
    tanh = jnp.tanh(inner)
    cdf = 0.5 + 0.5 * tanh
    slope = cdf + 0.5 * upper * (1.0 - tanh * tanh) * (scale + (3.0 * scale * 0.044715) * square)
    return upper * cdf, slope


def middle_kernel(dp_size, ring, n_exports, *refs):
    (
        tokens,
        att_ref,
        cotangent,
        seq_count,
        gain_ref,
        shift_ref,
        wo_own,
        wo_peer,
        up_own,
        down_own,
        up_peer,
        down_peer,
        layer_out,
        gmix_out,
        gheads_ref,
        og_own,
        og_peer,
        vec_ref,
    ) = refs[:18]
    exports = refs[18 : 18 + n_exports]
    (
        mixed_scr,
        stage_scr,
        two_scr,
        low_scr,
        two_t,
        low_t,
        act_scr,
        gup_scr,
        up_scr,
        down_scr,
        wo_scr,
        post_scr,
        grad_scr,
        local_sem,
        send_sem,
        recv_sem,
    ) = refs[18 + n_exports : 34 + n_exports]
    ring_scr = refs[34 + n_exports :]
    step = pl.program_id(0)
    steps = pl.num_programs(0)
    length, width = mixed_scr.shape
    blocks = length // BLOCK
    own_width = wo_own.shape[0]
    own_ff = up_own.shape[1]
    chunks = grad_scr.shape[0]
    ff_block = own_ff // chunks
    link = Link(dp_size)
    sems = (send_sem, recv_sem)
    rows_here = pl.ds(link.core * length, length)
    x_ref = gheads_ref
    loads = [
        pltpu.make_async_copy(tokens.at[rows_here], x_ref, local_sem.at[0]),
        pltpu.make_async_copy(wo_own, wo_scr.at[pl.ds(0, own_width)], local_sem.at[1]),
        pltpu.make_async_copy(wo_peer, wo_scr.at[pl.ds(own_width, own_width)], local_sem.at[2]),
        pltpu.make_async_copy(cotangent.at[rows_here], low_scr, local_sem.at[3]),
    ]
    weight_loads = [
        pltpu.make_async_copy(up_own, up_scr.at[:, pl.ds(0, own_ff)], local_sem.at[4]),
        pltpu.make_async_copy(up_peer, up_scr.at[:, pl.ds(own_ff, own_ff)], local_sem.at[5]),
        pltpu.make_async_copy(down_own, down_scr.at[pl.ds(0, own_ff)], local_sem.at[6]),
        pltpu.make_async_copy(down_peer, down_scr.at[pl.ds(own_ff, own_ff)], local_sem.at[7]),
    ]
    gmix_copy = pltpu.make_async_copy(mixed_scr, gmix_out, local_sem.at[8])

    def layer_copies(block):
        rows = pl.ds(link.core * length + block * BLOCK, BLOCK)
        return [
            pltpu.make_async_copy(
                stage_scr.at[lax.rem(block, 2)], layer_out.at[rows], local_sem.at[9 + block]
            ),
            remote(stage_scr.at[lax.rem(block, 2)], layer_out.at[rows], sems, block, link.peer),
        ]


    def swap(chunk):
        return remote(
            post_scr.at[lax.rem(chunk, 2)], grad_scr.at[chunk], sems, blocks + chunk, link.peer
        )

    flows = {}
    if ring:
        base = blocks + chunks
        hop1, hop2, deep1 = ring_scr
        for slot, chunk in enumerate((0, 2, 3, 5)):
            flows[chunk] = Chunk(
                link,
                sems,
                base + HOPS * chunk,
                grad_scr.at[chunk],
                hop1.at[slot],
                None if chunk else hop2,
            )
        flows[1] = DeepChunk(
            link, sems, base + HOPS, grad_scr.at[1], deep1, deep1.at[0], None, None, None
        )

    def run(events):
        for chunk, number in events:
            if ring:
                if number > 1:
                    flows[chunk].land(number - 1)
                flows[chunk].start(number)

    @pl.when(step == 0)
    def _():
        go(loads)
        go(weight_loads)
        partners = [link.peer]
        if ring:
            partners += [link.x_side, link.y_side]
            partners += [link.z_side(hop) for hop in range(1, link.depth)]
        link.meet(partners)
        finish(loads)
        live = jnp.where(link.core < seq_count[0], 1.0, 0.0).astype(F32)

        def enter(block):
            rows = row_block(block)
            mixed = x_ref[rows, :].astype(F32) + dot_nn(att_ref[rows, :], wo_scr[...])
            mixed_scr[rows, :] = mixed
            normed, _ = norm_stats(mixed)
            two_low = (normed * gain_ref[...] + shift_ref[...]).astype(BF16)
            two_scr[rows, :] = two_low
            two_t[:, rows] = jnp.transpose(two_low)
            low = (low_scr[rows, :].astype(F32) * live).astype(BF16)
            low_scr[rows, :] = low
            low_t[:, rows] = jnp.transpose(low)

        each(blocks, enter)
        finish(weight_loads)

    last = lax.div(step, steps - 1)
    mine = (1 - lax.rem(step, 2)) * lax.div(step + steps - 1, steps) + last
    mine_index = lax.div(step - 1 + lax.div(steps - step, steps), 2)
    post_index = lax.div(step + 1, 2)
    turn = mine * mine_index + (1 - mine) * (chunks + post_index)
    slot = 2 * mine + (1 - mine) * lax.rem(post_index, 2)
    cols = pl.ds(pl.multiple_of(turn * ff_block, ff_block), ff_block)
    for block in range(blocks):
        rows = slice(block * BLOCK, (block + 1) * BLOCK)
        upper = dot_nn(two_scr[rows, :], up_scr[:, cols])
        active, slope = gelu_pair(upper)
        act_scr[rows, cols] = active.astype(BF16)
        grad_active = dot_nt(low_scr[rows, :], down_scr[cols, :])
        gup_scr[rows, cols] = (grad_active * slope).astype(BF16)

    block_shape = grad_scr.shape[1:-1] + (ff_block,)
    @pl.when(jnp.logical_and(mine == 0, post_index > 1))
    def _():
        swap(post_index - 2).wait_send()

    post_scr[slot, ..., 0:ff_block] = dot_nn(low_t[...], act_scr[:, cols]).reshape(block_shape)
    post_scr[slot, ..., ff_block:] = dot_nn(two_t[...], gup_scr[:, cols]).reshape(block_shape)

    @pl.when(mine == 0)
    def _():
        swap(post_index).start()

    @pl.when(mine == 1)
    def _():
        swap(mine_index).wait_recv()
        grad_scr[mine_index] += post_scr[2]

    if ring:
        for when, events in {
            2: [(0, 1)],
            4: [(1, 1)],
            6: [(2, 1)],
            7: [(0, 2)],
            8: [(3, 1)],
        }.items():

            @pl.when(step == when)
            def _():
                run(events)

    @pl.when(step == steps - 1)
    def _():
        swap(chunks - 2).wait_send()
        swap(chunks - 1).wait_send()
        if not ring:
            whole_copy = pltpu.make_async_copy(grad_scr, exports[0], local_sem.at[13])
            whole_copy.start()

        def leave(block):
            rows = row_block(block)

            @pl.when(block > 1)
            def _():
                finish(layer_copies(block - 2))

            stage_scr[lax.rem(block, 2)] = mixed_scr[rows, :] + dot_nn(
                act_scr[rows, :], down_scr[...]
            )
            go(layer_copies(block))

        each(blocks, leave)
        run([(5, 1)])
        vec_ref[...] = jnp.zeros_like(vec_ref)

        def turn_back(block):
            rows = row_block(block)
            grad_two = dot_nt(gup_scr[rows, :], up_scr[...])
            normed, factor = norm_stats(mixed_scr[rows, :])
            vec_ref[0:1, :] += jnp.sum(grad_two * normed, axis=0, keepdims=True)
            vec_ref[1:2, :] += jnp.sum(grad_two, axis=0, keepdims=True)
            grad_mixed = low_scr[rows, :].astype(F32) + norm_backward(
                grad_two, normed, factor, gain_ref[...]
            )
            mixed_scr[rows, :] = grad_mixed
            grad_attn = grad_mixed.astype(BF16)
            low_t[:, rows] = jnp.transpose(grad_attn)
            gheads_ref[rows, :] = dot_nt(grad_attn, wo_scr[...]).astype(BF16)

        each(blocks, turn_back)
        gmix_copy.start()
        og_peer[...] = dot_nn(low_t[...], att_ref[:, own_width:]).reshape(og_peer.shape)
        og_own[...] = dot_nn(low_t[...], att_ref[:, 0:own_width]).reshape(og_own.shape)
        if ring:
            at_zero, at_one, at_two, at_deep = exports
            outs = [
                pltpu.make_async_copy(grad_scr.at[4], at_zero, local_sem.at[13]),
                pltpu.make_async_copy(hop1.at[pl.ds(1, 3)], at_one, local_sem.at[14]),
                pltpu.make_async_copy(hop2, at_two, local_sem.at[15]),
                pltpu.make_async_copy(deep1.at[0], at_deep, local_sem.at[16]),
            ]
            outs[0].start()
            flows[0].land(2)
            outs[2].start()
            flows[1].land(1)
            outs[3].start()
            flows[2].land(1)
            flows[3].land(1)
            flows[5].land(1)
            outs[1].start()
            finish(outs)
        else:
            whole_copy.wait()
        gmix_copy.wait()
        finish(layer_copies(blocks - 2))
        finish(layer_copies(blocks - 1))


def middle(
    dp_size, ring, tokens, attended, cotangent, seq_count, gain, shift, wo_own, wo_peer, own, peer
):
    width = tokens.shape[1]
    own_ff = own[0].shape[1]
    own_width = wo_own.shape[0]
    chunks = 6
    ff_block = own_ff // chunks
    grad_shape = place(ring, width, dp_size, 2 * ff_block)
    og_shape = place(ring, width, dp_size, own_width)
    scratch = []
    if ring:
        depth, rows = dp_size // 4, width // dp_size
        hop1 = (2, depth // 2, 2, rows, 2 * ff_block)
        hop2 = (depth, rows, 2 * ff_block)
        deep1 = (depth - 1, 2, 2, rows, 2 * ff_block)
        export_shapes = [grad_shape, (3,) + hop1, hop2, deep1[1:]]
        scratch = [
            pltpu.VMEM((4,) + hop1, F32),
            pltpu.VMEM(hop2, F32),
            pltpu.VMEM(deep1, F32),
        ]
    else:
        export_shapes = [(chunks,) + grad_shape]
    blocks = SEQ_LEN // BLOCK
    n_sems = blocks + chunks + HOPS * chunks
    return pl.pallas_call(
        functools.partial(middle_kernel, dp_size, ring, len(export_shapes)),
        grid=(2 * chunks,),
        in_specs=[
            ANY,
            fixed((SEQ_LEN, 2 * own_width)),
            ANY,
            SMEM,
            fixed((1, width)),
            fixed((1, width)),
            ANY,
            ANY,
            ANY,
            ANY,
            ANY,
            ANY,
        ],
        out_specs=[
            ANY,
            ANY,
            fixed((SEQ_LEN, 2 * own_width)),
            fixed(og_shape),
            fixed(og_shape),
            fixed((8, width)),
        ]
        + [ANY] * len(export_shapes),
        scratch_shapes=[
            pltpu.VMEM((SEQ_LEN, width), F32),
            pltpu.VMEM((2, BLOCK, width), F32),
            pltpu.VMEM((SEQ_LEN, width), BF16),
            pltpu.VMEM((SEQ_LEN, width), BF16),
            pltpu.VMEM((width, SEQ_LEN), BF16),
            pltpu.VMEM((width, SEQ_LEN), BF16),
            pltpu.VMEM((SEQ_LEN, 2 * own_ff), BF16),
            pltpu.VMEM((SEQ_LEN, 2 * own_ff), BF16),
            pltpu.VMEM((width, 2 * own_ff), BF16),
            pltpu.VMEM((2 * own_ff, width), BF16),
            pltpu.VMEM((2 * own_width, width), BF16),
            pltpu.VMEM((3,) + grad_shape, F32),
            pltpu.VMEM((chunks,) + grad_shape, F32),
            pltpu.SemaphoreType.DMA((17,)),
            pltpu.SemaphoreType.DMA((n_sems,)),
            pltpu.SemaphoreType.DMA((n_sems,)),
        ]
        + scratch,
        out_shape=[
            jax.ShapeDtypeStruct((2 * SEQ_LEN, width), F32),
            jax.ShapeDtypeStruct((SEQ_LEN, width), F32),
            jax.ShapeDtypeStruct((SEQ_LEN, 2 * own_width), BF16),
            jax.ShapeDtypeStruct(og_shape, F32),
            jax.ShapeDtypeStruct(og_shape, F32),
            jax.ShapeDtypeStruct((8, width), F32),
        ]
        + [jax.ShapeDtypeStruct(shape, F32) for shape in export_shapes],
        compiler_params=params(1),
        name="middle",
    )(tokens, attended, cotangent, seq_count, gain, shift, wo_own, wo_peer, *own, *peer)


def back_kernel(dp_size, ring, counts, *refs):
    n_in, n_out, fresh_width = counts
    (
        tokens,
        n1_ref,
        q_ref,
        k_ref,
        v_ref,
        att_ref,
        gheads_ref,
        lse_ref,
        gmix,
        gain_ref,
        w_ref,
        sel_ref,
        og_own,
        og_peer,
        vec2_ref,
    ) = refs[:15]
    exports = refs[15:n_in]
    in_grad, first_grad = refs[n_in : n_in + 2]
    outs = refs[n_in + 2 : n_in + n_out]
    scratch = refs[n_in + n_out :]
    (
        x_scr,
        gmix_scr,
        n1_t,
        dk_acc,
        dv_acc,
        dq_t,
        stack_scr,
        one_acc,
        fv_t,
        post_scr,
        out_scr,
        sums_scr,
        local_sem,
        send_sem,
        recv_sem,
    ) = scratch[:15]
    step = pl.program_id(0)
    steps = pl.num_programs(0)
    length, width = x_scr.shape
    blocks = length // BLOCK
    link = Link(dp_size)
    sems = (send_sem, recv_sem)
    rows_here = pl.ds(link.core * length, length)
    chunks = lse_ref.shape[0] * steps // 2
    grads = scratch[15 : 15 + chunks]
    ring_scr = list(scratch[15 + chunks :])
    side = fv_t.shape[0] // 2
    loads = [
        pltpu.make_async_copy(tokens.at[rows_here], x_scr, local_sem.at[0]),
        pltpu.make_async_copy(gmix, gmix_scr, local_sem.at[1]),
        pltpu.make_async_copy(og_own, out_scr.at[0], local_sem.at[2]),
    ]
    out_swap = remote(og_peer, out_scr.at[1], sems, 0, link.peer)
    swaps = [
        remote(
            post_scr.at[0, ..., pl.ds(0, grads[chunk].shape[-1])],
            grads[chunk],
            sems,
            1 + chunk,
            link.peer,
        )
        for chunk in range(chunks)
    ]
    base = 1 + chunks
    in_copies = [
        remote(one_acc, in_grad.at[rows_here], sems, base, link.peer),
        pltpu.make_async_copy(one_acc, in_grad.at[rows_here], local_sem.at[3]),
    ]
    seq_cols = pl.ds(pl.multiple_of(link.core * length, length), length)
    first_copies = [
        remote(
            fv_t.at[pl.ds((1 - link.core) * side, side)],
            first_grad.at[:, seq_cols],
            sems,
            base + 1,
            link.peer,
        ),
        pltpu.make_async_copy(
            fv_t.at[pl.ds(link.core * side, side)], first_grad.at[:, seq_cols], local_sem.at[4]
        ),
    ]
    base += 2
    flows = {}
    if ring:
        at_zero, at_one, at_two, at_deep = exports
        whole, hop1, hop2, hop3, deep, deep2, deep3 = ring_scr[:7]
        del ring_scr[:7]
        for slot, chunk in enumerate((0, 2, 3, 4, 5)):
            flows[chunk] = Chunk(
                link,
                sems,
                base + slot * HOPS,
                whole,
                None if chunk == 0 else hop1.at[slot - 1],
                hop2.at[slot],
                hop3.at[slot],
            )
        flows[0].sources[2] = at_two
        flows[2].sources[1] = at_one.at[0]
        flows[3].sources[1] = at_one.at[1]
        flows[4].sources[0] = at_zero
        flows[5].sources[1] = at_one.at[2]
        flows[1] = DeepChunk(
            link, sems, base + 5 * HOPS, None, None, deep, at_deep, deep2, deep3
        )
        ring_loads = [
            pltpu.make_async_copy(at_zero, whole, local_sem.at[5]),
            pltpu.make_async_copy(at_one.at[0], hop1.at[0], local_sem.at[6]),
            pltpu.make_async_copy(at_one.at[1], hop1.at[1], local_sem.at[7]),
            pltpu.make_async_copy(at_one.at[2], hop1.at[3], local_sem.at[8]),
            pltpu.make_async_copy(at_two, hop2.at[0], local_sem.at[9]),
            pltpu.make_async_copy(at_deep, deep, local_sem.at[10]),
        ]
        wholes = {"o": out_scr.at[0]}
        wholes.update({"p%d" % n: grads[n] for n in range(chunks)})
        place_in = base + 6 * HOPS
        for name, whole in wholes.items():
            flows[name] = Chunk(link, sems, place_in, whole, *ring_scr[:3])
            del ring_scr[:3]
            place_in += HOPS
        v_send, v_recv = ring_scr[:2]
        flows["v"] = Chunk(link, sems, place_in, v_recv, *ring_scr[2:5])
        vec_swap = remote(v_send, v_recv, sems, place_in + HOPS, link.peer)

    ready = [(1, 2), (2, 2)]

    def run(events):
        for name, number in events:
            if ring:
                if number > 1 and (name, number) not in ready:
                    flows[name].land(number - 1)
                flows[name].start(number)

    @pl.when(step == 0)
    def _():
        partners = [link.peer]
        if ring:
            partners += [link.x_side, link.y_side]
            partners += [link.z_side(hop) for hop in range(1, link.depth)]
        link.meet(partners)
        if ring:
            flows[3].start(2)
            flows[5].start(2)
            flows[0].start(3)
        out_swap.start()
        go(loads)
        if ring:
            go(ring_loads)
        for block in range(blocks):
            rows = slice(block * BLOCK, (block + 1) * BLOCK)
            n1_t[:, rows] = jnp.transpose(n1_ref[rows, :])
        one_acc[...] = jnp.zeros_like(one_acc)
        fv_t[...] = jnp.zeros_like(fv_t)

    k_t = jnp.transpose(k_ref[...])
    prod_t = jnp.transpose(gheads_ref[...].astype(F32) * att_ref[...].astype(F32))
    lse_pair = lse_ref[0]
    row_pos = lax.broadcasted_iota(jnp.int32, (BLOCK, BLOCK), 0)
    col_pos = lax.broadcasted_iota(jnp.int32, (BLOCK, BLOCK), 1)
    seen = row_pos <= col_pos
    for block in range(blocks):
        cols = slice(block * BLOCK, (block + 1) * BLOCK)
        queries = split_heads(q_ref[cols, :])
        heads_grad = split_heads(gheads_ref[cols, :])
        for head in range(2):
            part = slice(head * HEAD_DIM, (head + 1) * HEAD_DIM)
            delta = jnp.sum(prod_t[part, cols], axis=0, keepdims=True)
            lse = lse_pair[head : head + 1, cols]
            dq = jnp.zeros((HEAD_DIM, BLOCK), F32)
            for source in range(block + 1):
                rows = slice(source * BLOCK, (source + 1) * BLOCK)
                soft = jnp.exp(dot_nt(k_ref[rows, :], queries[head]) - lse)
                if source == block:
                    soft = jnp.where(seen, soft, 0.0)
                dsoft = dot_nt(v_ref[rows, :], heads_grad[head])
                dscore = (soft * (dsoft - delta)).astype(BF16)
                dv = dot_nn(soft.astype(BF16), heads_grad[head])
                dk = dot_nn(dscore, queries[head])
                if head == 0 and source == block:
                    dv_acc[rows, :] = dv
                    dk_acc[rows, :] = dk
                else:
                    dv_acc[rows, :] += dv
                    dk_acc[rows, :] += dk
                dq = dq + dot_nn(k_t[part, rows], dscore)
            dq_t[part, cols] = dq

    middle_events = {
        0: [(4, 1)],
        1: [(5, 3)],
        2: [(4, 2), (2, 3)],
        3: [("p0", 2)],
        4: [("p1", 1), ("p0", 3)],
        5: [("p1", 2)],
    }
    end_events = {
        0: [(2, 2), (3, 3)],
        1: [("p0", 1), (1, 2)],
        3: [("o", 1), (4, 3)],
        4: [("o", 2), (1, 3)],
        5: [("p2", 1), ("o", 3), ("p1", 3)],
    }
    if ring:
        for when, events in middle_events.items():

            @pl.when(step == when)
            def _():
                run(events)

        @pl.when(step == 0)
        def _():
            finish(ring_loads)

    for block in range(blocks):
        rows = slice(block * BLOCK, (block + 1) * BLOCK)
        stack_scr[rows, 0:PAIR] = (jnp.transpose(dq_t[:, rows]) * HEAD_DIM**-0.5).astype(BF16)
        stack_scr[rows, PAIR : 2 * PAIR] = dk_acc[rows, :].astype(BF16)
        dv = dv_acc[rows, :]
        stack_scr[rows, 2 * PAIR : 3 * PAIR] = dv.astype(BF16)
        one_acc[rows, :] += dot_nt(stack_scr[rows, :], w_ref[...])

    @pl.when(step >= 2 * (fresh_width // PAIR))
    def _():
        for block in range(blocks):
            rows = slice(block * BLOCK, (block + 1) * BLOCK)
            dv = dv_acc[rows, :]
            high = dv.astype(BF16)
            low = (dv - high.astype(F32)).astype(BF16)
            fv_t[:, rows] += dot_nt(sel_ref[...], high) + dot_nt(sel_ref[...], low)

    for chunk in range(1, chunks):

        @pl.when(step == 2 * chunk)
        def _():
            swaps[chunk - 1].wait_send()

    post_scr[lax.rem(step, 2)] = dot_nn(n1_t[...], stack_scr[...]).reshape(post_scr.shape[1:])
    for chunk in range(chunks):
        used = grads[chunk].shape[-1]

        @pl.when(step == 2 * chunk)
        def _():
            swaps[chunk].start()

        @pl.when(step == 2 * chunk + 1)
        def _():
            swaps[chunk].wait_recv()
            grads[chunk][...] += post_scr[1, ..., 0:used]
            if chunk == chunks - 1:
                swaps[chunk].wait_send()

    @pl.when(step == 0)
    def _():
        out_swap.wait()
        finish(loads)
        out_scr[0] += out_scr[1]

    if ring:
        for when, events in end_events.items():

            @pl.when(step == when)
            def _():
                run(events)

    @pl.when(step == steps - 1)
    def _():
        go(first_copies)
        sums_scr[...] = jnp.zeros_like(sums_scr)

        def leave(block):
            rows = row_block(block)
            normed, factor = norm_stats(x_scr[rows, :].astype(F32))
            grad_one = one_acc[rows, :]
            sums_scr[0:1, :] += jnp.sum(grad_one * normed, axis=0, keepdims=True)
            sums_scr[1:2, :] += jnp.sum(grad_one, axis=0, keepdims=True)
            one_acc[rows, :] = gmix_scr[rows, :] + norm_backward(
                grad_one, normed, factor, gain_ref[...]
            )

        each(blocks, leave)
        go(in_copies)
        vectors = jnp.concatenate(
            [sums_scr[0:2, :], vec2_ref[0:2, :], jnp.zeros((4, width), F32)], axis=0
        )
        if ring:
            up_out, down_out, q_out, k_out, v_out, o_out, vec_out = outs
            rows_dev = width // dp_size
            v_send[...] = jnp.zeros_like(v_send)
            for block in range(dp_size):
                v_send[block // 4, (block // 2) % 2, block % 2, :, 0:rows_dev] = vectors[
                    :, block * rows_dev : (block + 1) * rows_dev
                ]
            vec_swap.start()
            run([("p2", 2)])
            vec_swap.wait()
            v_recv[...] += v_send[...]
            run([("v", 1)])
            ff_block = up_out.shape[-1] // 6

            def put_ffn(index, total):
                cols = slice(index * ff_block, (index + 1) * ff_block)
                down_out[:, cols] = total[:, 0:ff_block]
                up_out[:, cols] = total[:, ff_block:]

            def put_proj(index, total):
                cols = slice(index * PAIR, (index + 1) * PAIR)
                q_out[:, cols] = total[:, 0:PAIR]
                k_out[:, cols] = total[:, PAIR : 2 * PAIR]
                if total.shape[1] > 2 * PAIR:
                    last = min((index + 1) * PAIR, fresh_width)
                    v_out[:, index * PAIR : last] = total[
                        :, 2 * PAIR : 2 * PAIR + last - index * PAIR
                    ]

            for chunk in range(6):
                put_ffn(chunk, flows[chunk].total())
            o_out[...] = flows["o"].total()
            run([("v", 2), ("p2", 3), ("v", 3)])
            put_proj(0, flows["p0"].total())
            put_proj(1, flows["p1"].total())
            put_proj(2, flows["p2"].total())
            vec_out[...] = flows["v"].total()
        else:
            vec_out = outs[-1]
            vec_out[...] = vectors
            stores = [
                pltpu.make_async_copy(grads[chunk], outs[chunk], local_sem.at[5 + chunk])
                for chunk in range(chunks)
            ]
            stores.append(pltpu.make_async_copy(out_scr.at[0], outs[chunks], local_sem.at[8]))
            go(stores)
            finish(stores)
        finish(in_copies)
        finish(first_copies)


def back(
    dp_size,
    ring,
    tokens,
    n1,
    q,
    k,
    v,
    attended,
    grad_heads,
    lse,
    grad_mixed,
    gain,
    weights,
    select,
    og_own,
    og_peer,
    vec2,
    exports,
    fresh_width,
    own_ff,
):
    width = tokens.shape[1]
    own_width = og_own.shape[-1]
    half = own_width // PAIR
    fv_width = select.shape[0]
    side = fv_width // 2
    pair_of = lambda i: lax.rem(i + 1, 2) * half + lax.div(i, 2)
    pair_block = pl.BlockSpec((SEQ_LEN, PAIR), lambda i: (0, pair_of(i)))
    used = [3 * PAIR if n * PAIR < fresh_width else 2 * PAIR for n in range(half)]
    grad_shapes = [place(ring, width, dp_size, columns) for columns in used]
    og_shape = place(ring, width, dp_size, own_width)
    scratch = [
        pltpu.VMEM((SEQ_LEN, width), BF16),
        pltpu.VMEM((SEQ_LEN, width), F32),
        pltpu.VMEM((width, SEQ_LEN), BF16),
        pltpu.VMEM((SEQ_LEN, PAIR), F32),
        pltpu.VMEM((SEQ_LEN, PAIR), F32),
        pltpu.VMEM((PAIR, SEQ_LEN), F32),
        pltpu.VMEM((SEQ_LEN, 3 * PAIR), BF16),
        pltpu.VMEM((SEQ_LEN, width), F32),
        pltpu.VMEM((fv_width, SEQ_LEN), F32),
        pltpu.VMEM((2,) + grad_shapes[0], F32),
        pltpu.VMEM((2,) + og_shape, F32),
        pltpu.VMEM((8, width), F32),
        pltpu.SemaphoreType.DMA((11,)),
    ]
    n_sems = 3 + half + (1 + (8 + half) * HOPS if ring else 0)
    scratch += [pltpu.SemaphoreType.DMA((n_sems,))] * 2
    scratch += [pltpu.VMEM(shape, F32) for shape in grad_shapes]
    if ring:
        depth, rows = dp_size // 4, width // dp_size

        def hops(columns, first, height=rows):
            shapes = [
                (2, depth // 2, 2, height, columns),
                (depth, height, columns),
                (depth - 1, height, columns),
            ]
            return [pltpu.VMEM(shape, F32) for shape in shapes[first:]]

        ff = exports[0].shape[-1]
        scratch += [
            pltpu.VMEM(place(ring, width, dp_size, ff), F32),
            pltpu.VMEM((4, 2, depth // 2, 2, rows, ff), F32),
            pltpu.VMEM((5, depth, rows, ff), F32),
            pltpu.VMEM((5, depth - 1, rows, ff), F32),
            pltpu.VMEM((2, 2, rows, ff), F32),
            pltpu.VMEM((2, 2, rows, ff // 2), F32),
            pltpu.VMEM((2, rows, ff // 2), F32),
        ]
        scratch += hops(own_width, 0)
        for columns in used:
            scratch += hops(columns, 0)
        vec_whole = pltpu.VMEM((depth, 2, 2, 8, PAIR), F32)
        scratch += [vec_whole, vec_whole] + hops(PAIR, 0, 8)
        totals = [
            (rows, own_ff),
            (rows, own_ff),
            (rows, own_width),
            (rows, own_width),
            (rows, fresh_width),
            (rows, own_width),
            (8, PAIR),
        ]
        total_specs = [fixed(shape) for shape in totals]
        export_args = list(exports)
        export_specs = [ANY] * len(export_args)
    else:
        totals = grad_shapes + [og_shape, (8, width)]
        total_specs = [ANY] * (half + 1) + [fixed((8, width))]
        export_args, export_specs = [], []
    in_specs = [
        ANY,
        fixed((SEQ_LEN, width)),
        pair_block,
        pair_block,
        pair_block,
        pair_block,
        pair_block,
        pl.BlockSpec((1, 8, SEQ_LEN), lambda i: (pair_of(i), 0, 0)),
        ANY,
        fixed((1, width)),
        pl.BlockSpec((width, 3 * PAIR), lambda i: (0, pair_of(i))),
        pl.BlockSpec((fv_width, PAIR), lambda i: (0, pair_of(i))),
        ANY,
        ANY,
        fixed((8, width)),
    ] + export_specs
    return pl.pallas_call(
        functools.partial(
            back_kernel, dp_size, ring, (len(in_specs), 2 + len(totals), fresh_width)
        ),
        grid=(2 * half,),
        in_specs=in_specs,
        out_specs=[ANY, ANY] + total_specs,
        scratch_shapes=scratch,
        out_shape=[
            jax.ShapeDtypeStruct((2 * SEQ_LEN, width), F32),
            jax.ShapeDtypeStruct((side, 2 * SEQ_LEN), F32),
        ]
        + [jax.ShapeDtypeStruct(shape, F32) for shape in totals],
        compiler_params=params(2),
        name="back",
    )(
        tokens,
        n1,
        q,
        k,
        v,
        attended,
        grad_heads,
        lse,
        grad_mixed,
        gain,
        weights,
        select,
        og_own,
        og_peer,
        vec2,
        *export_args,
    )


def on_device(
    dp_size,
    tokens,
    first_values,
    seq_count,
    skip_map,
    norm1_gain,
    norm1_shift,
    query_weight,
    key_weight,
    value_weight,
    out_weight,
    norm2_gain,
    norm2_shift,
    up_weight,
    down_weight,
    cotangent,
):
    width = tokens.shape[1]
    own_width = query_weight.shape[1]
    fresh_width = value_weight.shape[1]
    own_ff = up_weight.shape[1]
    ring = ring_of(dp_size, width)
    gain1, shift1 = norm1_gain[None, :], norm1_shift[None, :]
    gain2, shift2 = norm2_gain[None, :], norm2_shift[None, :]
    n1, q, k, v, attended, lse, weights, select, out_peer, up_peer, down_peer = front(
        dp_size,
        tokens,
        first_values,
        skip_map,
        gain1,
        shift1,
        query_weight,
        key_weight,
        value_weight.T,
        out_weight,
        up_weight,
        down_weight,
    )
    layer_out, grad_mixed, grad_heads, og_own, og_peer, vec2, *exports = middle(
        dp_size,
        ring,
        tokens,
        attended,
        cotangent,
        seq_count,
        gain2,
        shift2,
        out_weight,
        out_peer,
        (up_weight, down_weight),
        (up_peer, down_peer),
    )
    input_grad, first_grad, *totals = back(
        dp_size,
        ring,
        tokens,
        n1,
        q,
        k,
        v,
        attended,
        grad_heads,
        lse,
        grad_mixed,
        gain1,
        weights,
        select,
        og_own,
        og_peer,
        vec2,
        exports,
        fresh_width,
        own_ff,
    )
    first_grad = first_grad.T
    if ring:
        up_total, down_t, query_total, key_total, value_total, out_t, vectors = totals
        rows = width // dp_size
        down_total, out_total = down_t.T, out_t.T
        gain1_total, shift1_total, gain2_total, shift2_total = (vectors[n, :rows] for n in range(4))
    else:
        *proj, out_grad, vectors = totals
        chunks = exports[0].shape[0]
        ff_block = own_ff // chunks
        vectors = vectors + lax.ppermute(vectors, "tensor", [(0, 1), (1, 0)])
        columns = list(proj) + [out_grad] + [exports[0][n] for n in range(chunks)]
        packed = jnp.concatenate(columns + [jnp.pad(vectors.T, ((0, 0), (0, 120)))], axis=1)
        summed = lax.psum_scatter(packed, "dp", scatter_dimension=0, tiled=True)
        heads, start = [[], [], []], 0
        for part in proj:
            for n in range(part.shape[1] // PAIR):
                heads[n].append(summed[:, start : start + PAIR])
                start += PAIR
        query_total, key_total, value_total = (jnp.concatenate(part, axis=1) for part in heads)
        value_total = value_total[:, :fresh_width]
        out_total = summed[:, start : start + own_width].T
        start += own_width
        pairs = summed[:, start : start + 2 * own_ff].reshape(-1, chunks, 2, ff_block)
        down_total = pairs[:, :, 0].reshape(-1, own_ff).T
        up_total = pairs[:, :, 1].reshape(-1, own_ff)
        start += 2 * own_ff
        gain1_total, shift1_total, gain2_total, shift2_total = (
            summed[:, start + n] for n in range(4)
        )
    return (
        layer_out,
        input_grad,
        first_grad,
        gain1_total,
        shift1_total,
        query_total,
        key_total,
        value_total,
        out_total,
        gain2_total,
        shift2_total,
        up_total,
        down_total,
    )


def solution(mesh):
    placed = (
        P("dp", None),
        P("dp", None),
        P("dp"),
        P("tensor"),
        P(),
        P(),
        P(None, "tensor"),
        P(None, "tensor"),
        P(None, "tensor"),
        P("tensor", None),
        P(),
        P(),
        P(None, "tensor"),
        P("tensor", None),
        P("dp", None),
    )
    return jax.shard_map(
        functools.partial(on_device, mesh.shape["dp"]),
        mesh=mesh,
        in_specs=placed,
        out_specs=(
            P("dp", None),
            P("dp", None),
            P("dp", "tensor"),
            P("dp"),
            P("dp"),
            P("dp", "tensor"),
            P("dp", "tensor"),
            P("dp", "tensor"),
            P("tensor", "dp"),
            P("dp"),
            P("dp"),
            P("dp", "tensor"),
            P("tensor", "dp"),
        ),
        check_vma=False,
    )
```

profile of v0, /device:TPU:0, one launch (start us, length us, event | category | flops | bytes accessed | tf_op | source)
XLA Modules:
  0.0 201.7 jit_solution(4899663910442888899)
XLA Ops:
  0.6 1.3 broadcast_in_dim.12.gain_ref.refs_9_
  1.9 1.3 broadcast_in_dim.13.shift_ref
  3.2 0.0 copy-start.8
  3.2 0.0 copy-start.9
  3.2 37.0 %front.1 = (bf16[1024,768]{1,0:T(8,128)(2,1)}, bf16[1024,768]{1,0:T(8,128)(2,1)}, bf16[1024,768]{1,0:T(8,128)(2,1)}, bf16[1024,768]{1,0:T(8,128)(2,1)}, bf16[102...) custom-call(bf16[2048,768]{1,0:T(8,128)(2,1)} %refs_0_.3, ...), custom_call_target="tpu_custom_call" | custom-call | tf_op jit(solution)/shard_map/front/pallas_call | solution.py:517
  40.9 0.0 copy-done.8
  40.9 0.6 broadcast_in_dim.14.refs_4_
  41.5 0.0 copy-done.9
  41.5 0.6 broadcast_in_dim.15.refs_5_
  42.0 63.4 %middle.1 = (f32[2048,768]{1,0:T(8,128)}, f32[1024,768]{1,0:T(8,128)}, bf16[1024,768]{1,0:T(8,128)(2,1)}, f32[4,2,2,48,384]{4,3,2,1,0:T(8,128)}, f32[4,2,2,48,38...) custom-call(bf16[2048,768]{1,0:T(8,128)(2,1)} %refs_0_.3, ...), custom_call_target="tpu_custom_call" | custom-call | tf_op jit(solution)/shard_map/middle/pallas_call | solution.py:867
  105.5 80.9 %back.1 = (f32[2048,768]{1,0:T(8,128)}, f32[192,2048]{1,0:T(8,128)}, f32[48,1536]{1,0:T(8,128)}, f32[48,1536]{1,0:T(8,128)}, f32[48,384]{1,0:T(8,128)}, /*index=...) custom-call(bf16[2048,768]{1,0:T(8,128)(2,1)} %refs_0_.3, ...), custom_call_target="tpu_custom_call" | custom-call | tf_op jit(solution)/shard_map/back/pallas_call | solution.py:1375
  186.4 1.4 slice_bitcast_fusion
  187.8 6.1 %copy.38 = f32[2048,768]{1,0:T(8,128)} copy(f32[2048,768]{1,0:T(8,128)} %get-tuple-element.90) | data formatting | bytes 12582912
  193.8 0.0 copy-done
  193.8 2.7 %copy.39 = f32[2048,768]{1,0:T(8,128)} copy(f32[2048,768]{1,0:T(8,128)S(1)} %copy-done) | data formatting | bytes 12582912
  196.5 0.0 copy-done.1
  196.5 0.0 copy-start.4
  196.6 0.0 copy-start.3
  196.6 0.0 copy-start.2
  196.6 1.1 copy.40
  197.7 0.0 copy-done.6
  197.7 0.6 copy.41
  198.4 0.0 copy-done.5
  198.4 0.6 copy.42
  199.0 0.0 copy-done.7
  199.0 0.6 copy.43
  199.6 0.0 copy-done.4
  199.6 0.6 copy.44
  200.3 0.0 copy-done.3
  200.3 0.7 copy.45
  201.0 0.0 copy-done.2
  201.0 0.7 copy.46
  (5 shorter events, 0.0 us)
Async XLA Ops:
  3.2 37.7 %copy-start.8 = (f32[768]{0:T(1024)S(1)}, f32[768]{0:T(1024)}, u32[]{:S(2)}) copy-start(f32[768]{0:T(1024)} %param.25) | copy-start | bytes 9220
  3.2 38.3 %copy-start.9 = (f32[768]{0:T(1024)S(1)}, f32[768]{0:T(1024)}, u32[]{:S(2)}) copy-start(f32[768]{0:T(1024)} %param.26) | copy-start | bytes 9220
  187.8 6.1 %copy-start = (f32[2048,768]{1,0:T(8,128)S(1)}, f32[2048,768]{1,0:T(8,128)}, u32[]{:S(2)}) copy-start(f32[2048,768]{1,0:T(8,128)} %get-tuple-element.91) | copy-start | bytes 18874372
  193.8 2.7 %copy-start.1 = (f32[192,2048]{1,0:T(8,128)S(1)}, f32[192,2048]{1,0:T(8,128)}, u32[]{:S(2)}) copy-start(f32[192,2048]{1,0:T(8,128)} %get-tuple-element.65) | copy-start | bytes 4718596
  196.5 1.2 copy-start.6
  196.5 1.8 copy-start.5
  196.5 2.5 %copy-start.7 = (f32[48,192]{1,0:T(8,128)S(1)}, f32[48,192]{1,0:T(8,128)}, u32[]{:S(2)}) copy-start(f32[48,192]{1,0:T(8,128)} %get-tuple-element.97) | copy-start | bytes 110596
  196.5 3.1 %copy-start.4 = (f32[48,384]{1,0:T(8,128)S(1)}, f32[48,384]{1,0:T(8,128)}, u32[]{:S(2)}) copy-start(f32[48,384]{1,0:T(8,128)} %get-tuple-element.70) | copy-start | bytes 221188
  196.6 3.7 %copy-start.3 = (f32[48,1536]{1,0:T(8,128)S(1)}, f32[48,1536]{1,0:T(8,128)}, u32[]{:S(2)}) copy-start(f32[48,1536]{1,0:T(8,128)} %get-tuple-element.101) | copy-start | bytes 884740
  196.6 4.4 %copy-start.2 = (f32[48,1536]{1,0:T(8,128)S(1)}, f32[48,1536]{1,0:T(8,128)}, u32[]{:S(2)}) copy-start(f32[48,1536]{1,0:T(8,128)} %get-tuple-element.72) | copy-start | bytes 884740
where the time goes:
time: 202 us
  Pallas kernels  181 us (90%)
  local copies, waits for them, and re-layouts  18.9 us (9%)
    pallas_call x1, Pallas kernels, back(): pl.pallas_call(functools.partial(back_kernel, dp_size, ring, (len(in_spec...  80.9 us
    pallas_call x1, Pallas kernels, middle(): pl.pallas_call(functools.partial(middle_kernel, dp_size, ring, len(export...  63.4 us
    pallas_call x1, Pallas kernels, front(): pl.pallas_call(functools.partial(front_kernel, dp_size), grid=(2 * half,)...  37 us
    unnamed x29, local copies, waits for them, and re-layouts  13.9 us

commit v1 on v0

--- a/solution.py
+++ b/solution.py
@@ -13,7 +13,6 @@
 PAIR = 2 * HEAD_DIM
 EPS = 1e-05
 FILL = -1e30
-VMEM_BYTES = 60 * 1024 * 1024
 
 F32 = jnp.float32
 BF16 = jnp.bfloat16
@@ -72,9 +71,11 @@
 MESH = pl.DeviceIdType.MESH
 
 
-def params(collective_id):
+def params(collective_id, vmem_mib):
     return pltpu.CompilerParams(
-        vmem_limit_bytes=VMEM_BYTES, collective_id=collective_id, has_side_effects=True
+        vmem_limit_bytes=vmem_mib * 1024 * 1024,
+        collective_id=collective_id,
+        has_side_effects=True,
     )
 
 
@@ -116,11 +117,13 @@
     def z_side(self, hop):
         return {"dp": 4 * self.z_place(hop) + lax.rem(self.dp, 4)}
 
-    def meet(self, partners):
+    def greet(self, partners):
         barrier = pltpu.get_barrier_semaphore()
         for partner in partners:
             pl.semaphore_signal(barrier, inc=1, device_id=partner, device_id_type=MESH)
-        pl.semaphore_wait(barrier, len(partners))
+
+    def meet(self, partners):
+        pl.semaphore_wait(pltpu.get_barrier_semaphore(), len(partners))
 
 
 def remote(source, target, sems, index, device):
@@ -392,6 +395,7 @@
 
     @pl.when(step == 0)
     def _():
+        link.greet([link.peer])
         go(local)
         proj_own[2, :, 0:fresh_width] = jnp.transpose(wv_ref[...])
         proj_own[2, :, fresh_width:] = jnp.zeros((width, own_width - fresh_width), BF16)
@@ -419,7 +423,7 @@
         def one(block, carry):
             rows = pl.ds(block * BLOCK, BLOCK)
             normed, _ = norm_stats(x_scr[rows, :].astype(F32))
-            n1_ref[rows, :] = (normed * gain_ref[...] + shift_ref[...]).astype(BF16)
+            n1_ref[rows, :] = (normed * gain_ref[...][None, :] + shift_ref[...][None, :]).astype(BF16)
             return carry
 
         lax.fori_loop(0, blocks, one, 0)
@@ -454,31 +458,57 @@
     row_pos = lax.broadcasted_iota(jnp.int32, (BLOCK, BLOCK), 0)
     col_pos = lax.broadcasted_iota(jnp.int32, (BLOCK, BLOCK), 1)
     seen = col_pos <= row_pos
-    for block in range(blocks):
+    items = [(block, head) for block in range(blocks) for head in range(2)]
+    scores, weights, partial = {}, {}, {}
+
+    def score(index):
+        block, head = items[index]
         lo, hi = block * BLOCK, (block + 1) * BLOCK
-        queries = split_heads(q_ref[lo:hi, :])
-        total = jnp.zeros((BLOCK, PAIR), F32)
-        lse_tile = lse_scr[lo:hi, :]
-        for head in range(2):
-            diag = jnp.where(seen, dot_nt(queries[head], k_ref[lo:hi, :]), FILL)
-            peak = jnp.max(diag, axis=-1, keepdims=True)
-            if block:
-                past = dot_nt(queries[head], k_ref[0:lo, :])
-                peak = jnp.maximum(peak, jnp.max(past, axis=-1, keepdims=True))
-            diag = jnp.exp(diag - peak)
-            mass = jnp.sum(diag, axis=-1, keepdims=True)
-            if block:
-                past = jnp.exp(past - peak)
-                mass = mass + jnp.sum(past, axis=-1, keepdims=True)
-            inverse = 1.0 / mass
-            total = total + dot_nn((diag * inverse).astype(BF16), split_heads(v_ref[lo:hi, :])[head])
-            if block:
-                total = total + dot_nn(
-                    (past * inverse).astype(BF16), split_heads(v_ref[0:lo, :])[head]
-                )
-            lse_tile = jnp.where(lane == 2 * step + head, peak + jnp.log(mass), lse_tile)
-        att_ref[lo:hi, :] = total.astype(BF16)
-        lse_scr[lo:hi, :] = lse_tile
+        query = split_heads(q_ref[lo:hi, :])[head]
+        diag = dot_nt(query, k_ref[lo:hi, :])
+        scores[index] = (diag, dot_nt(query, k_ref[0:lo, :]) if block else None)
+
+    def soften(index):
+        block, head = items[index]
+        lo, hi = block * BLOCK, (block + 1) * BLOCK
+        diag, past = scores.pop(index)
+        diag = jnp.where(seen, diag, FILL)
+        peak = jnp.max(diag, axis=-1, keepdims=True)
+        if block:
+            peak = jnp.maximum(peak, jnp.max(past, axis=-1, keepdims=True))
+        diag = jnp.exp(diag - peak)
+        mass = jnp.sum(diag, axis=-1, keepdims=True)
+        if block:
+            past = jnp.exp(past - peak)
+            mass = mass + jnp.sum(past, axis=-1, keepdims=True)
+        inverse = 1.0 / mass
+        weights[index] = (
+            (diag * inverse).astype(BF16),
+            (past * inverse).astype(BF16) if block else None,
+        )
+        lse_scr[lo:hi, :] = jnp.where(
+            lane == 2 * step + head, peak + jnp.log(mass), lse_scr[lo:hi, :]
+        )
+
+    def attend(index):
+        block, head = items[index]
+        lo, hi = block * BLOCK, (block + 1) * BLOCK
+        diag, past = weights.pop(index)
+        total = dot_nn(diag, split_heads(v_ref[lo:hi, :])[head])
+        if block:
+            total = total + dot_nn(past, split_heads(v_ref[0:lo, :])[head])
+        if head == 0:
+            partial[block] = total
+        else:
+            att_ref[lo:hi, :] = (partial.pop(block) + total).astype(BF16)
+
+    for index in range(len(items) + 2):
+        if index < len(items):
+            score(index)
+        if 0 <= index - 1 < len(items):
+            soften(index - 1)
+        if index >= 2:
+            attend(index - 2)
 
     @pl.when(step == 0)
     def _():
@@ -521,8 +551,8 @@
             ANY,
             ANY,
             SMEM,
-            fixed((1, width)),
-            fixed((1, width)),
+            fixed((width,)),
+            fixed((width,)),
             fixed(wq.shape),
             fixed(wk.shape),
             fixed(wv.shape),
@@ -578,7 +608,7 @@
             jax.ShapeDtypeStruct(up_w.shape, BF16),
             jax.ShapeDtypeStruct(down_w.shape, BF16),
         ],
-        compiler_params=params(0),
+        compiler_params=params(0, 60),
         name="front",
     )(tokens, first_values, skip_map, gain, shift, wq, wk, wv, out_w, up_w, down_w)
 
@@ -692,6 +722,11 @@
             link, sems, base + HOPS, grad_scr.at[1], deep1, deep1.at[0], None, None, None
         )
 
+    partners = [link.peer]
+    if ring:
+        partners += [link.x_side, link.y_side]
+        partners += [link.z_side(hop) for hop in range(1, link.depth)]
+
     def run(events):
         for chunk, number in events:
             if ring:
@@ -701,13 +736,9 @@
 
     @pl.when(step == 0)
     def _():
+        link.greet(partners)
         go(loads)
         go(weight_loads)
-        partners = [link.peer]
-        if ring:
-            partners += [link.x_side, link.y_side]
-            partners += [link.z_side(hop) for hop in range(1, link.depth)]
-        link.meet(partners)
         finish(loads)
         live = jnp.where(link.core < seq_count[0], 1.0, 0.0).astype(F32)
 
@@ -716,7 +747,7 @@
             mixed = x_ref[rows, :].astype(F32) + dot_nn(att_ref[rows, :], wo_scr[...])
             mixed_scr[rows, :] = mixed
             normed, _ = norm_stats(mixed)
-            two_low = (normed * gain_ref[...] + shift_ref[...]).astype(BF16)
+            two_low = (normed * gain_ref[...][None, :] + shift_ref[...][None, :]).astype(BF16)
             two_scr[rows, :] = two_low
             two_t[:, rows] = jnp.transpose(two_low)
             low = (low_scr[rows, :].astype(F32) * live).astype(BF16)
@@ -725,6 +756,7 @@
 
         each(blocks, enter)
         finish(weight_loads)
+        link.meet(partners)
 
     last = lax.div(step, steps - 1)
     mine = (1 - lax.rem(step, 2)) * lax.div(step + steps - 1, steps) + last
@@ -802,7 +834,7 @@
             vec_ref[0:1, :] += jnp.sum(grad_two * normed, axis=0, keepdims=True)
             vec_ref[1:2, :] += jnp.sum(grad_two, axis=0, keepdims=True)
             grad_mixed = low_scr[rows, :].astype(F32) + norm_backward(
-                grad_two, normed, factor, gain_ref[...]
+                grad_two, normed, factor, gain_ref[...][None, :]
             )
             mixed_scr[rows, :] = grad_mixed
             grad_attn = grad_mixed.astype(BF16)
@@ -872,8 +904,8 @@
             fixed((SEQ_LEN, 2 * own_width)),
             ANY,
             SMEM,
-            fixed((1, width)),
-            fixed((1, width)),
+            fixed((width,)),
+            fixed((width,)),
             ANY,
             ANY,
             ANY,
@@ -918,7 +950,7 @@
             jax.ShapeDtypeStruct((8, width), F32),
         ]
         + [jax.ShapeDtypeStruct(shape, F32) for shape in export_shapes],
-        compiler_params=params(1),
+        compiler_params=params(1, 60),
         name="middle",
     )(tokens, attended, cotangent, seq_count, gain, shift, wo_own, wo_peer, *own, *peer)
 
@@ -1066,6 +1098,7 @@
         if ring:
             partners += [link.x_side, link.y_side]
             partners += [link.z_side(hop) for hop in range(1, link.depth)]
+        link.greet(partners)
         link.meet(partners)
         if ring:
             flows[3].start(2)
@@ -1087,32 +1120,61 @@
     row_pos = lax.broadcasted_iota(jnp.int32, (BLOCK, BLOCK), 0)
     col_pos = lax.broadcasted_iota(jnp.int32, (BLOCK, BLOCK), 1)
     seen = row_pos <= col_pos
-    for block in range(blocks):
+    items = [
+        (block, head, source)
+        for block in range(blocks)
+        for head in range(2)
+        for source in range(block + 1)
+    ]
+    raw, soft_low, dq_sums = {}, {}, {}
+
+    def part_of(ref, block, head):
+        return split_heads(ref[block * BLOCK : (block + 1) * BLOCK, :])[head]
+
+    def score(index):
+        block, head, source = items[index]
+        rows = slice(source * BLOCK, (source + 1) * BLOCK)
+        raw[index] = (
+            dot_nt(k_ref[rows, :], part_of(q_ref, block, head)),
+            dot_nt(v_ref[rows, :], part_of(gheads_ref, block, head)),
+        )
+
+    def soften(index):
+        block, head, source = items[index]
         cols = slice(block * BLOCK, (block + 1) * BLOCK)
-        queries = split_heads(q_ref[cols, :])
-        heads_grad = split_heads(gheads_ref[cols, :])
-        for head in range(2):
-            part = slice(head * HEAD_DIM, (head + 1) * HEAD_DIM)
-            delta = jnp.sum(prod_t[part, cols], axis=0, keepdims=True)
-            lse = lse_pair[head : head + 1, cols]
-            dq = jnp.zeros((HEAD_DIM, BLOCK), F32)
-            for source in range(block + 1):
-                rows = slice(source * BLOCK, (source + 1) * BLOCK)
-                soft = jnp.exp(dot_nt(k_ref[rows, :], queries[head]) - lse)
-                if source == block:
-                    soft = jnp.where(seen, soft, 0.0)
-                dsoft = dot_nt(v_ref[rows, :], heads_grad[head])
-                dscore = (soft * (dsoft - delta)).astype(BF16)
-                dv = dot_nn(soft.astype(BF16), heads_grad[head])
-                dk = dot_nn(dscore, queries[head])
-                if head == 0 and source == block:
-                    dv_acc[rows, :] = dv
-                    dk_acc[rows, :] = dk
-                else:
-                    dv_acc[rows, :] += dv
-                    dk_acc[rows, :] += dk
-                dq = dq + dot_nn(k_t[part, rows], dscore)
-            dq_t[part, cols] = dq
+        part = slice(head * HEAD_DIM, (head + 1) * HEAD_DIM)
+        delta = jnp.sum(prod_t[part, cols], axis=0, keepdims=True)
+        scores, dsoft = raw.pop(index)
+        soft = jnp.exp(scores - lse_pair[head : head + 1, cols])
+        if source == block:
+            soft = jnp.where(seen, soft, 0.0)
+        soft_low[index] = (soft.astype(BF16), (soft * (dsoft - delta)).astype(BF16))
+
+    def spread(index):
+        block, head, source = items[index]
+        rows = slice(source * BLOCK, (source + 1) * BLOCK)
+        part = slice(head * HEAD_DIM, (head + 1) * HEAD_DIM)
+        soft, dscore = soft_low.pop(index)
+        dv = dot_nn(soft, part_of(gheads_ref, block, head))
+        dk = dot_nn(dscore, part_of(q_ref, block, head))
+        if head == 0 and source == block:
+            dv_acc[rows, :] = dv
+            dk_acc[rows, :] = dk
+        else:
+            dv_acc[rows, :] += dv
+            dk_acc[rows, :] += dk
+        dq = dot_nn(k_t[part, rows], dscore)
+        dq_sums[block, head] = dq if source == 0 else dq_sums[block, head] + dq
+        if source == block:
+            dq_t[part, block * BLOCK : (block + 1) * BLOCK] = dq_sums.pop((block, head))
+
+    for index in range(len(items) + 2):
+        if index < len(items):
+            score(index)
+        if 0 <= index - 1 < len(items):
+            soften(index - 1)
+        if index >= 2:
+            spread(index - 2)
 
     middle_events = {
         0: [(4, 1)],
@@ -1203,7 +1265,7 @@
             sums_scr[0:1, :] += jnp.sum(grad_one * normed, axis=0, keepdims=True)
             sums_scr[1:2, :] += jnp.sum(grad_one, axis=0, keepdims=True)
             one_acc[rows, :] = gmix_scr[rows, :] + norm_backward(
-                grad_one, normed, factor, gain_ref[...]
+                grad_one, normed, factor, gain_ref[...][None, :]
             )
 
         each(blocks, leave)
@@ -1365,7 +1427,7 @@
         pair_block,
         pl.BlockSpec((1, 8, SEQ_LEN), lambda i: (pair_of(i), 0, 0)),
         ANY,
-        fixed((1, width)),
+        fixed((width,)),
         pl.BlockSpec((width, 3 * PAIR), lambda i: (0, pair_of(i))),
         pl.BlockSpec((fv_width, PAIR), lambda i: (0, pair_of(i))),
         ANY,
@@ -1385,7 +1447,7 @@
             jax.ShapeDtypeStruct((side, 2 * SEQ_LEN), F32),
         ]
         + [jax.ShapeDtypeStruct(shape, F32) for shape in totals],
-        compiler_params=params(2),
+        compiler_params=params(2, 60),
         name="back",
     )(
         tokens,
@@ -1405,6 +1467,36 @@
         vec2,
         *export_args,
     )
+
+
+def collect_kernel(large, *refs):
+    half = len(refs) // 2
+    pairs = list(zip(refs[:half], refs[half:]))
+    for source, target in pairs[:large]:
+        target[...] = source[...]
+
+    @pl.when(pl.program_id(0) == 0)
+    def _():
+        for source, target in pairs[large:]:
+            target[...] = source[...]
+
+
+def collect(tall, columns, small):
+    blocks = 8
+    rows = tall[0]
+    specs = [pl.BlockSpec((rows.shape[0] // blocks, rows.shape[1]), lambda i: (i, 0))] * 2 + [
+        pl.BlockSpec((columns.shape[0], columns.shape[1] // blocks), lambda i: (0, i)),
+    ] + [fixed(array.shape) for array in small]
+    arrays = tall + [columns] + small
+    return pl.pallas_call(
+        functools.partial(collect_kernel, 3),
+        grid=(blocks,),
+        in_specs=specs,
+        out_specs=specs,
+        out_shape=[jax.ShapeDtypeStruct(array.shape, array.dtype) for array in arrays],
+        compiler_params=pltpu.CompilerParams(vmem_limit_bytes=60 * 1024 * 1024),
+        name="collect",
+    )(*arrays)
 
 
 def on_device(
@@ -1430,8 +1522,7 @@
     fresh_width = value_weight.shape[1]
     own_ff = up_weight.shape[1]
     ring = ring_of(dp_size, width)
-    gain1, shift1 = norm1_gain[None, :], norm1_shift[None, :]
-    gain2, shift2 = norm2_gain[None, :], norm2_shift[None, :]
+    gain1, shift1, gain2, shift2 = norm1_gain, norm1_shift, norm2_gain, norm2_shift
     n1, q, k, v, attended, lse, weights, select, out_peer, up_peer, down_peer = front(
         dp_size,
         tokens,
@@ -1482,9 +1573,10 @@
         fresh_width,
         own_ff,
     )
-    first_grad = first_grad.T
     if ring:
-        up_total, down_t, query_total, key_total, value_total, out_t, vectors = totals
+        *totals, vectors = totals
+        layer_out, input_grad, first_grad, *totals = collect([layer_out, input_grad], first_grad, totals)
+        up_total, down_t, query_total, key_total, value_total, out_t = totals
         rows = width // dp_size
         down_total, out_total = down_t.T, out_t.T
         gain1_total, shift1_total, gain2_total, shift2_total = (vectors[n, :rows] for n in range(4))
@@ -1515,7 +1607,7 @@
     return (
         layer_out,
         input_grad,
-        first_grad,
+        first_grad.T,
         gain1_total,
         shift1_total,
         query_total,

time: 202 us -> 190 us (0.941)
  local copies, waits for them, and re-layouts: 18.9 us -> 0.53 us
  Pallas kernels: 181 us -> 187 us
    unnamed x29 -> x2, local copies, waits for them, and re-layouts: 13.9 us -> 0.01 us
    pallas_call x0 -> x1, Pallas kernels: none -> 12.8 us  [collect(): pl.pallas_call(functools.partial(collect_kernel, 3), grid=(blocks,), in_s...]
    pallas_call x1, Pallas kernels: 37 us -> 30.7 us  [front(): pl.pallas_call(functools.partial(front_kernel, dp_size), grid=(2 * half,)...]
    broadcast_in_dim x4 -> x0, local copies, waits for them, and re-layouts: 3.7 us -> none  [the longest x2 2.53 us: on_device(): gain1, shift1 = (norm1_gain[None, :], norm1_shift[None, :])]
where the time goes in v1:
time: 190 us; the launch traced here: 189 us
  Pallas kernels  187 us (98%)
    pallas_call x1, Pallas kernels, back(): pl.pallas_call(functools.partial(back_kernel, dp_size, ring, (len(in_spec...  81.5 us
    pallas_call x1, Pallas kernels, middle(): pl.pallas_call(functools.partial(middle_kernel, dp_size, ring, len(export...  62.4 us
    pallas_call x1, Pallas kernels, front(): pl.pallas_call(functools.partial(front_kernel, dp_size), grid=(2 * half,)...  30.7 us
    pallas_call x1, Pallas kernels, collect(): pl.pallas_call(functools.partial(collect_kernel, 3), grid=(blocks,), in_s...  12.8 us

profile of v1, /device:TPU:0, one launch (start us, length us, event | category | flops | bytes accessed | tf_op | source)
XLA Modules:
  0.0 189.3 jit_solution(9597320157393818706)
XLA Ops:
  0.6 30.7 %front.1 = (bf16[1024,768]{1,0:T(8,128)(2,1)}, bf16[1024,768]{1,0:T(8,128)(2,1)}, bf16[1024,768]{1,0:T(8,128)(2,1)}, bf16[1024,768]{1,0:T(8,128)(2,1)}, bf16[102...) custom-call(bf16[2048,768]{1,0:T(8,128)(2,1)} %refs_0_.3, ...), custom_call_target="tpu_custom_call" | custom-call | tf_op jit(solution)/shard_map/front/pallas_call | solution.py:547
  32.0 62.4 %middle.1 = (f32[2048,768]{1,0:T(8,128)}, f32[1024,768]{1,0:T(8,128)}, bf16[1024,768]{1,0:T(8,128)(2,1)}, f32[4,2,2,48,384]{4,3,2,1,0:T(8,128)}, f32[4,2,2,48,38...) custom-call(bf16[2048,768]{1,0:T(8,128)(2,1)} %refs_0_.3, ...), custom_call_target="tpu_custom_call" | custom-call | tf_op jit(solution)/shard_map/middle/pallas_call | solution.py:899
  94.4 81.5 %back.1 = (f32[2048,768]{1,0:T(8,128)}, f32[192,2048]{1,0:T(8,128)}, f32[48,1536]{1,0:T(8,128)}, f32[48,1536]{1,0:T(8,128)}, f32[48,384]{1,0:T(8,128)}, /*index=...) custom-call(bf16[2048,768]{1,0:T(8,128)(2,1)} %refs_0_.3, ...), custom_call_target="tpu_custom_call" | custom-call | tf_op jit(solution)/shard_map/back/pallas_call | solution.py:1437
  175.9 0.0 copy-start
  175.9 12.8 %collect.1 = (f32[2048,768]{1,0:T(8,128)}, f32[2048,768]{1,0:T(8,128)}, f32[192,2048]{1,0:T(8,128)}, f32[48,1536]{1,0:T(8,128)}, f32[48,1536]{1,0:T(8,128)}, /*i...) custom-call(f32[2048,768]{1,0:T(8,128)} %get-tuple-element.56.refs_0_, ...), custom_call_target="tpu_custom_call" | custom-call | tf_op jit(solution)/shard_map/collect/pallas_call | solution.py:1491
  188.7 0.0 copy-done
  188.7 0.5 slice_bitcast_fusion
Async XLA Ops:
  175.9 12.8 %copy-start = (f32[8,128]{1,0:T(8,128)S(1)}, f32[8,128]{1,0:T(8,128)}, u32[]{:S(2)}) copy-start(f32[8,128]{1,0:T(8,128)} %get-tuple-element.84) | copy-start | bytes 12292

commit v2 on v1

--- a/solution.py
+++ b/solution.py
@@ -89,33 +89,28 @@
 
 
 def ring_of(dp_size, width):
-    rows = width // dp_size
-    return dp_size % 8 == 0 and width % dp_size == 0 and rows % 8 == 0
+    return dp_size == 4 * 4 and width % (8 * dp_size) == 0
 
 
 def place(ring, width, dp_size, columns):
     if not ring:
         return (width, columns)
-    return (dp_size // 4, 2, 2, width // dp_size, columns)
+    return (2, 2, 2, 2, width // dp_size, columns)
 
 
 class Link:
     def __init__(self, dp_size):
         self.dp = lax.axis_index("dp")
         self.core = lax.axis_index("tensor")
-        self.depth = dp_size // 4
         self.x = lax.rem(self.dp, 2)
         self.y = lax.rem(lax.div(self.dp, 2), 2)
-        self.z = lax.div(self.dp, 4)
+        self.z_low = lax.rem(lax.div(self.dp, 4), 2)
+        self.z_high = lax.rem(lax.div(self.dp, 8), 2)
         self.peer = {"tensor": 1 - self.core}
         self.x_side = {"dp": self.dp + 1 - 2 * self.x}
         self.y_side = {"dp": self.dp + 2 - 4 * self.y}
-
-    def z_place(self, hop):
-        return lax.rem(self.z + hop, self.depth)
-
-    def z_side(self, hop):
-        return {"dp": 4 * self.z_place(hop) + lax.rem(self.dp, 4)}
+        self.z_side = {"dp": self.dp + 4 - 8 * self.z_low}
+        self.z_far = {"dp": self.dp + 8 - 16 * self.z_high}
 
     def greet(self, partners):
         barrier = pltpu.get_barrier_semaphore()
@@ -138,55 +133,6 @@
     )
 
 
-def first_hop(link, source, landing, sems, base):
-    low = link.depth // 2
-    return [
-        remote(
-            source.at[0:low, :, 1 - link.x], landing.at[0], sems, base, link.x_side
-        ),
-        remote(
-            source.at[low : 2 * low, 1 - link.y],
-            landing.at[1],
-            sems,
-            base + 1,
-            link.y_side,
-        ),
-    ]
-
-
-def second_hop(link, source, landing, sems, base):
-    low = link.depth // 2
-    return [
-        remote(
-            source.at[0, :, 1 - link.y],
-            landing.at[0:low],
-            sems,
-            base,
-            link.y_side,
-        ),
-        remote(
-            source.at[1, :, 1 - link.x],
-            landing.at[low : 2 * low],
-            sems,
-            base + 1,
-            link.x_side,
-        ),
-    ]
-
-
-def last_hop(link, source, landing, sems, base):
-    return [
-        remote(
-            source.at[link.z_place(hop)],
-            landing.at[hop - 1],
-            sems,
-            base + hop - 1,
-            link.z_side(hop),
-        )
-        for hop in range(1, link.depth)
-    ]
-
-
 def go(copies):
     for copy in copies:
         copy.start()
@@ -197,94 +143,33 @@
         copy.wait()
 
 
-def merge_first(link, whole, landing):
-    low = link.depth // 2
-
-    def one(row):
-        for other in range(2):
-            landing[0, row, other] += whole[row, other, link.x]
-            landing[1, row, other] += whole[low + row, link.y, other]
-
-    each(low, one)
-
-
-def merge_second(link, landed, landing):
-    low = link.depth // 2
-
-    def one(row):
-        landing[row] += landed[0, row, link.y]
-        landing[low + row] += landed[1, row, link.x]
-
-    each(low, one)
-
-
-def total_last(own, landing):
-    total = own
-    for hop in range(landing.shape[0]):
-        total = total + landing[hop]
-    return total
-
-
-HOPS = 7
+HOPS = 6
 
 
 class Chunk:
-    def __init__(self, link, sems, base, whole=None, hop1=None, hop2=None, hop3=None):
-        self.link, self.whole, self.hop1, self.hop2, self.hop3 = link, whole, hop1, hop2, hop3
-        self.sems, self.base = sems, base
-        self.sources = [whole, hop1, hop2]
-
-    def hop(self, number):
-        source = self.sources[number - 1]
-        if number == 1:
-            return first_hop(self.link, source, self.hop1, self.sems, self.base)
-        if number == 2:
-            return second_hop(self.link, source, self.hop2, self.sems, self.base + 2)
-        return last_hop(self.link, source, self.hop3, self.sems, self.base + 4)
-
-    def start(self, number):
-        go(self.hop(number))
-
-    def land(self, number):
-        finish(self.hop(number))
-        if number == 1:
-            merge_first(self.link, self.whole, self.hop1)
-        elif number == 2:
-            merge_second(self.link, self.hop1, self.hop2)
-
-    def total(self):
-        finish(self.hop(3))
-        return total_last(self.hop2[self.link.z], self.hop3)
-
-
-class DeepChunk:
-    def __init__(self, link, sems, base, whole, hop1, summed, source, hop2, hop3):
-        self.link, self.whole, self.hop1, self.hop2, self.hop3 = link, whole, hop1, hop2, hop3
-        self.summed, self.source = summed, source
-        self.sems, self.base = sems, base
+    def __init__(self, link, sems, base, whole, hop1, hop2=None, hop3=None, hop4=None):
+        self.link, self.sems, self.base = link, sems, base
+        self.held = [whole, hop1, hop2, hop3, hop4]
+        self.sources = list(self.held)
 
     def hop(self, number):
         link, sems, base = self.link, self.sems, self.base
+        source, landing = self.sources[number - 1], self.held[number]
         if number == 1:
-            return last_hop(link, self.whole, self.hop1, sems, base)
-        side = self.hop3.shape[-1]
-        left, right = pl.ds(0, side), pl.ds(side, side)
+            return [
+                remote(source.at[0, :, :, 1 - link.x], landing.at[0], sems, base, link.x_side),
+                remote(source.at[1, :, 1 - link.y], landing.at[1], sems, base + 1, link.y_side),
+            ]
         if number == 2:
-            base += link.depth - 1
-            summed = self.source
             return [
-                remote(
-                    summed.at[:, 1 - link.x, :, left], self.hop2.at[0], sems, base, link.x_side
-                ),
-                remote(
-                    summed.at[1 - link.y, :, :, right], self.hop2.at[1], sems, base + 1, link.y_side
-                ),
+                remote(source.at[0, :, 1 - link.y], landing.at[0], sems, base + 2, link.y_side),
+                remote(source.at[1, :, 1 - link.x], landing.at[1], sems, base + 3, link.x_side),
             ]
-        base += link.depth + 1
-        return [
-            remote(self.hop2.at[0, 1 - link.y], self.hop3.at[0], sems, base, link.y_side),
-            remote(self.hop2.at[1, 1 - link.x], self.hop3.at[1], sems, base + 1, link.x_side),
-        ]
+        if number == 3:
+            return [
+                remote(source.at[:, 1 - link.z_low], landing, sems, base + 4, link.z_side)
+            ]
+        return [remote(source.at[1 - link.z_high], landing, sems, base + 5, link.z_far)]
 
     def start(self, number):
         go(self.hop(number))
@@ -292,28 +177,93 @@
     def land(self, number):
         link = self.link
         finish(self.hop(number))
+        own, landing = self.held[number - 1], self.held[number]
+
+        def one(row):
+            if number == 1:
+                for other in range(2):
+                    landing[0, row, other] += own[0, row, other, link.x]
+                    landing[1, row, other] += own[1, row, link.y, other]
+            elif number == 2:
+                landing[0, row] += own[0, row, link.y]
+                landing[1, row] += own[1, row, link.x]
+            else:
+                landing[row] += own[row, link.z_low]
+
+        each(2, one)
+
+    def total(self):
+        finish(self.hop(4))
+        return self.held[3][self.link.z_high] + self.held[4][...]
+
+
+class DeepChunk:
+    def __init__(self, link, sems, base, whole, hop1, hop2=None, hop3=None, hop4=None):
+        self.link, self.sems, self.base = link, sems, base
+        self.held = [whole, hop1, hop2, hop3, hop4]
+        self.sources = list(self.held)
+
+    def hop(self, number):
+        link, sems, base = self.link, self.sems, self.base
+        source, landing = self.sources[number - 1], self.held[number]
         if number == 1:
-
-            def one(row):
+            return [remote(source.at[:, 1 - link.z_low], landing, sems, base, link.z_side)]
+        if number == 2:
+            return [remote(source.at[1 - link.z_high], landing, sems, base + 1, link.z_far)]
+        if number == 3:
+            side = landing.shape[-1]
+            left, right = pl.ds(0, side), pl.ds(side, side)
+            return [
+                remote(
+                    source.at[:, 1 - link.x, :, left], landing.at[0], sems, base + 2, link.x_side
+                ),
+                remote(
+                    source.at[1 - link.y, :, :, right], landing.at[1], sems, base + 3, link.y_side
+                ),
+            ]
+        return [
+            remote(source.at[0, 1 - link.y], landing.at[0], sems, base + 4, link.y_side),
+            remote(source.at[1, 1 - link.x], landing.at[1], sems, base + 5, link.x_side),
+        ]
+
+    def start(self, number):
+        go(self.hop(number))
+
+    def land(self, number):
+        link = self.link
+        finish(self.hop(number))
+        own, landing = self.held[number - 1], self.held[number]
+
+        def one(row):
+            if number == 1:
+                for other in range(4):
+                    y, x = other // 2, other % 2
+                    landing[row, y, x] += own[row, link.z_low, y, x]
+            elif number == 2:
                 for other in range(2):
-                    total = self.whole[link.z, row, other]
-                    for hop in range(self.hop1.shape[0]):
-                        total = total + self.hop1[hop, row, other]
-                    self.summed[row, other] = total
-
-            each(2, one)
-        else:
-            side = self.hop3.shape[-1]
-            for other in range(2):
-                self.hop2[0, other] += self.summed[other, link.x, :, 0:side]
-                self.hop2[1, other] += self.summed[link.y, other, :, side:]
+                    landing[row, other] += own[row, other]
+            else:
+                side = landing.shape[-1]
+                landing[0, row] += own[row, link.x, :, 0:side]
+                landing[1, row] += own[link.y, row, :, side:]
+
+        each(2, one)
 
     def total(self):
-        finish(self.hop(3))
+        finish(self.hop(4))
+        own, landed = self.held[3], self.held[4]
         return jnp.concatenate(
-            [self.hop2[0, self.link.y] + self.hop3[0], self.hop2[1, self.link.x] + self.hop3[1]],
-            axis=-1,
+            [own[0, self.link.y] + landed[0], own[1, self.link.x] + landed[1]], axis=-1
         )
+
+
+def hop_shapes(rows, columns):
+    return [
+        (2, 2, 2, rows, columns),
+        (2, 2, rows, columns),
+        (2, rows, columns),
+        (rows, columns),
+    ]
 
 
 def front_kernel(
@@ -626,7 +576,7 @@
 def middle_kernel(dp_size, ring, n_exports, *refs):
     (
         tokens,
-        att_ref,
+        attended,
         cotangent,
         seq_count,
         gain_ref,
@@ -646,6 +596,7 @@
     ) = refs[:18]
     exports = refs[18 : 18 + n_exports]
     (
+        att_ref,
         mixed_scr,
         stage_scr,
         two_scr,
@@ -662,8 +613,8 @@
         local_sem,
         send_sem,
         recv_sem,
-    ) = refs[18 + n_exports : 34 + n_exports]
-    ring_scr = refs[34 + n_exports :]
+    ) = refs[18 + n_exports : 35 + n_exports]
+    ring_scr = refs[35 + n_exports :]
     step = pl.program_id(0)
     steps = pl.num_programs(0)
     length, width = mixed_scr.shape
@@ -681,6 +632,7 @@
         pltpu.make_async_copy(wo_own, wo_scr.at[pl.ds(0, own_width)], local_sem.at[1]),
         pltpu.make_async_copy(wo_peer, wo_scr.at[pl.ds(own_width, own_width)], local_sem.at[2]),
         pltpu.make_async_copy(cotangent.at[rows_here], low_scr, local_sem.at[3]),
+        pltpu.make_async_copy(attended, att_ref, local_sem.at[16]),
     ]
     weight_loads = [
         pltpu.make_async_copy(up_own, up_scr.at[:, pl.ds(0, own_ff)], local_sem.at[4]),
@@ -709,7 +661,7 @@
     if ring:
         base = blocks + chunks
         hop1, hop2, deep1 = ring_scr
-        for slot, chunk in enumerate((0, 2, 3, 5)):
+        for slot, chunk in enumerate((0, 2, 4, 5)):
             flows[chunk] = Chunk(
                 link,
                 sems,
@@ -718,14 +670,14 @@
                 hop1.at[slot],
                 None if chunk else hop2,
             )
-        flows[1] = DeepChunk(
-            link, sems, base + HOPS, grad_scr.at[1], deep1, deep1.at[0], None, None, None
-        )
+        for slot, chunk in enumerate((1, 3)):
+            flows[chunk] = DeepChunk(
+                link, sems, base + HOPS * chunk, grad_scr.at[chunk], deep1.at[slot]
+            )
 
     partners = [link.peer]
     if ring:
-        partners += [link.x_side, link.y_side]
-        partners += [link.z_side(hop) for hop in range(1, link.depth)]
+        partners += [link.x_side, link.y_side, link.z_side]
 
     def run(events):
         for chunk, number in events:
@@ -795,8 +747,9 @@
             2: [(0, 1)],
             4: [(1, 1)],
             6: [(2, 1)],
-            7: [(0, 2)],
-            8: [(3, 1)],
+            8: [(3, 1), (0, 2)],
+            10: [(4, 1)],
+            11: [(5, 1)],
         }.items():
 
             @pl.when(step == when)
@@ -824,7 +777,6 @@
             go(layer_copies(block))
 
         each(blocks, leave)
-        run([(5, 1)])
         vec_ref[...] = jnp.zeros_like(vec_ref)
 
         def turn_back(block):
@@ -846,22 +798,21 @@
         og_peer[...] = dot_nn(low_t[...], att_ref[:, own_width:]).reshape(og_peer.shape)
         og_own[...] = dot_nn(low_t[...], att_ref[:, 0:own_width]).reshape(og_own.shape)
         if ring:
-            at_zero, at_one, at_two, at_deep = exports
+            at_one, at_two, at_deep = exports
             outs = [
-                pltpu.make_async_copy(grad_scr.at[4], at_zero, local_sem.at[13]),
-                pltpu.make_async_copy(hop1.at[pl.ds(1, 3)], at_one, local_sem.at[14]),
-                pltpu.make_async_copy(hop2, at_two, local_sem.at[15]),
-                pltpu.make_async_copy(deep1.at[0], at_deep, local_sem.at[16]),
+                pltpu.make_async_copy(hop1.at[pl.ds(1, 3)], at_one, local_sem.at[13]),
+                pltpu.make_async_copy(hop2, at_two, local_sem.at[14]),
+                pltpu.make_async_copy(deep1, at_deep, local_sem.at[15]),
             ]
+            flows[0].land(2)
+            outs[1].start()
+            flows[1].land(1)
+            flows[3].land(1)
+            outs[2].start()
+            flows[2].land(1)
+            flows[5].land(1)
+            flows[4].land(1)
             outs[0].start()
-            flows[0].land(2)
-            outs[2].start()
-            flows[1].land(1)
-            outs[3].start()
-            flows[2].land(1)
-            flows[3].land(1)
-            flows[5].land(1)
-            outs[1].start()
             finish(outs)
         else:
             whole_copy.wait()
@@ -882,15 +833,12 @@
     og_shape = place(ring, width, dp_size, own_width)
     scratch = []
     if ring:
-        depth, rows = dp_size // 4, width // dp_size
-        hop1 = (2, depth // 2, 2, rows, 2 * ff_block)
-        hop2 = (depth, rows, 2 * ff_block)
-        deep1 = (depth - 1, 2, 2, rows, 2 * ff_block)
-        export_shapes = [grad_shape, (3,) + hop1, hop2, deep1[1:]]
+        hop1, hop2, _, _ = hop_shapes(width // dp_size, 2 * ff_block)
+        export_shapes = [(3,) + hop1, hop2, (2,) + hop1]
         scratch = [
             pltpu.VMEM((4,) + hop1, F32),
             pltpu.VMEM(hop2, F32),
-            pltpu.VMEM(deep1, F32),
+            pltpu.VMEM((2,) + hop1, F32),
         ]
     else:
         export_shapes = [(chunks,) + grad_shape]
@@ -901,7 +849,7 @@
         grid=(2 * chunks,),
         in_specs=[
             ANY,
-            fixed((SEQ_LEN, 2 * own_width)),
+            ANY,
             ANY,
             SMEM,
             fixed((width,)),
@@ -923,6 +871,7 @@
         ]
         + [ANY] * len(export_shapes),
         scratch_shapes=[
+            pltpu.VMEM((SEQ_LEN, 2 * own_width), BF16),
             pltpu.VMEM((SEQ_LEN, width), F32),
             pltpu.VMEM((2, BLOCK, width), F32),
             pltpu.VMEM((SEQ_LEN, width), BF16),
@@ -1043,47 +992,53 @@
     base += 2
     flows = {}
     if ring:
-        at_zero, at_one, at_two, at_deep = exports
-        whole, hop1, hop2, hop3, deep, deep2, deep3 = ring_scr[:7]
-        del ring_scr[:7]
-        for slot, chunk in enumerate((0, 2, 3, 4, 5)):
+        at_one, at_two, at_deep = exports
+        hop1, hop2, hop3, hop4, deep1, deep2, deep3, deep4 = ring_scr[:8]
+        del ring_scr[:8]
+        for slot, chunk in enumerate((0, 2, 4, 5)):
             flows[chunk] = Chunk(
                 link,
                 sems,
                 base + slot * HOPS,
-                whole,
+                None,
                 None if chunk == 0 else hop1.at[slot - 1],
                 hop2.at[slot],
                 hop3.at[slot],
+                hop4.at[slot],
             )
+            if chunk:
+                flows[chunk].sources[1] = at_one.at[slot - 1]
         flows[0].sources[2] = at_two
-        flows[2].sources[1] = at_one.at[0]
-        flows[3].sources[1] = at_one.at[1]
-        flows[4].sources[0] = at_zero
-        flows[5].sources[1] = at_one.at[2]
-        flows[1] = DeepChunk(
-            link, sems, base + 5 * HOPS, None, None, deep, at_deep, deep2, deep3
-        )
+        for slot, chunk in enumerate((1, 3)):
+            flows[chunk] = DeepChunk(
+                link,
+                sems,
+                base + (4 + slot) * HOPS,
+                None,
+                deep1.at[slot],
+                deep2.at[slot],
+                deep3.at[slot],
+                deep4.at[slot],
+            )
+            flows[chunk].sources[1] = at_deep.at[slot]
         ring_loads = [
-            pltpu.make_async_copy(at_zero, whole, local_sem.at[5]),
-            pltpu.make_async_copy(at_one.at[0], hop1.at[0], local_sem.at[6]),
-            pltpu.make_async_copy(at_one.at[1], hop1.at[1], local_sem.at[7]),
-            pltpu.make_async_copy(at_one.at[2], hop1.at[3], local_sem.at[8]),
-            pltpu.make_async_copy(at_two, hop2.at[0], local_sem.at[9]),
-            pltpu.make_async_copy(at_deep, deep, local_sem.at[10]),
+            pltpu.make_async_copy(at_one, hop1, local_sem.at[5]),
+            pltpu.make_async_copy(at_two, hop2.at[0], local_sem.at[6]),
+            pltpu.make_async_copy(at_deep.at[0, link.z_high], deep1.at[0], local_sem.at[7]),
+            pltpu.make_async_copy(at_deep.at[1, link.z_high], deep1.at[1], local_sem.at[8]),
         ]
         wholes = {"o": out_scr.at[0]}
         wholes.update({"p%d" % n: grads[n] for n in range(chunks)})
         place_in = base + 6 * HOPS
         for name, whole in wholes.items():
-            flows[name] = Chunk(link, sems, place_in, whole, *ring_scr[:3])
-            del ring_scr[:3]
+            flows[name] = Chunk(link, sems, place_in, whole, *ring_scr[:4])
+            del ring_scr[:4]
             place_in += HOPS
         v_send, v_recv = ring_scr[:2]
-        flows["v"] = Chunk(link, sems, place_in, v_recv, *ring_scr[2:5])
+        flows["v"] = Chunk(link, sems, place_in, v_recv, *ring_scr[2:6])
         vec_swap = remote(v_send, v_recv, sems, place_in + HOPS, link.peer)
 
-    ready = [(1, 2), (2, 2)]
+    ready = [(1, 2), (2, 2), (3, 2), (4, 2), (5, 2), (0, 3)]
 
     def run(events):
         for name, number in events:
@@ -1096,11 +1051,11 @@
     def _():
         partners = [link.peer]
         if ring:
-            partners += [link.x_side, link.y_side]
-            partners += [link.z_side(hop) for hop in range(1, link.depth)]
+            partners += [link.x_side, link.y_side, link.z_side, link.z_far]
         link.greet(partners)
         link.meet(partners)
         if ring:
+            flows[2].start(2)
             flows[3].start(2)
             flows[5].start(2)
             flows[0].start(3)
@@ -1177,19 +1132,18 @@
             spread(index - 2)
 
     middle_events = {
-        0: [(4, 1)],
-        1: [(5, 3)],
-        2: [(4, 2), (2, 3)],
-        3: [("p0", 2)],
-        4: [("p1", 1), ("p0", 3)],
-        5: [("p1", 2)],
+        2: [(5, 3)],
+        3: [(3, 3), (4, 3)],
+        4: [("o", 3), (5, 4)],
+        5: [("p1", 2), (4, 4)],
     }
     end_events = {
-        0: [(2, 2), (3, 3)],
-        1: [("p0", 1), (1, 2)],
-        3: [("o", 1), (4, 3)],
-        4: [("o", 2), (1, 3)],
-        5: [("p2", 1), ("o", 3), ("p1", 3)],
+        0: [("o", 1)],
+        1: [("p0", 1), (1, 2), (4, 2), (2, 3)],
+        2: [("o", 2)],
+        3: [("p1", 1)],
+        4: [("p0", 2)],
+        5: [("p2", 1), ("p0", 3), (0, 4), (2, 4), ("o", 4)],
     }
     if ring:
         for when, events in middle_events.items():
@@ -1278,14 +1232,16 @@
             rows_dev = width // dp_size
             v_send[...] = jnp.zeros_like(v_send)
             for block in range(dp_size):
-                v_send[block // 4, (block // 2) % 2, block % 2, :, 0:rows_dev] = vectors[
+                v_send[block // 8, block // 4 % 2, block // 2 % 2, block % 2, :, 0:rows_dev] = vectors[
                     :, block * rows_dev : (block + 1) * rows_dev
                 ]
             vec_swap.start()
             run([("p2", 2)])
             vec_swap.wait()
             v_recv[...] += v_send[...]
-            run([("v", 1)])
+            run(
+                [("v", 1), (1, 3), ("p1", 3), ("p2", 3), ("v", 2), (1, 4), (3, 4), ("p0", 4), ("p1", 4), ("v", 3), ("p2", 4), ("v", 4)]
+            )
             ff_block = up_out.shape[-1] // 6
 
             def put_ffn(index, total):
@@ -1306,7 +1262,6 @@
             for chunk in range(6):
                 put_ffn(chunk, flows[chunk].total())
             o_out[...] = flows["o"].total()
-            run([("v", 2), ("p2", 3), ("v", 3)])
             put_proj(0, flows["p0"].total())
             put_proj(1, flows["p1"].total())
             put_proj(2, flows["p2"].total())
@@ -1376,31 +1331,22 @@
     scratch += [pltpu.SemaphoreType.DMA((n_sems,))] * 2
     scratch += [pltpu.VMEM(shape, F32) for shape in grad_shapes]
     if ring:
-        depth, rows = dp_size // 4, width // dp_size
-
-        def hops(columns, first, height=rows):
-            shapes = [
-                (2, depth // 2, 2, height, columns),
-                (depth, height, columns),
-                (depth - 1, height, columns),
-            ]
-            return [pltpu.VMEM(shape, F32) for shape in shapes[first:]]
+        rows = width // dp_size
+
+        def hops(columns, height=rows, count=None):
+            lead = () if count is None else (count,)
+            return [lead + shape for shape in hop_shapes(height, columns)]
 
         ff = exports[0].shape[-1]
-        scratch += [
-            pltpu.VMEM(place(ring, width, dp_size, ff), F32),
-            pltpu.VMEM((4, 2, depth // 2, 2, rows, ff), F32),
-            pltpu.VMEM((5, depth, rows, ff), F32),
-            pltpu.VMEM((5, depth - 1, rows, ff), F32),
-            pltpu.VMEM((2, 2, rows, ff), F32),
-            pltpu.VMEM((2, 2, rows, ff // 2), F32),
-            pltpu.VMEM((2, rows, ff // 2), F32),
-        ]
-        scratch += hops(own_width, 0)
+        shapes = [(3,) + hops(ff)[0]] + hops(ff, count=4)[1:]
+        shapes += [(2, 2, 2, rows, ff)] * 2
+        shapes += [(2, 2, 2, rows, ff // 2), (2, 2, rows, ff // 2)]
+        shapes += hops(own_width)
         for columns in used:
-            scratch += hops(columns, 0)
-        vec_whole = pltpu.VMEM((depth, 2, 2, 8, PAIR), F32)
-        scratch += [vec_whole, vec_whole] + hops(PAIR, 0, 8)
+            shapes += hops(columns)
+        vec_whole = place(ring, width, dp_size, PAIR)[:4] + (8, PAIR)
+        shapes += [vec_whole, vec_whole] + hops(PAIR, 8)
+        scratch += [pltpu.VMEM(shape, F32) for shape in shapes]
         totals = [
             (rows, own_ff),
             (rows, own_ff),

time: 190 us -> 185 us (0.974)
  Pallas kernels: 187 us -> 181 us
    pallas_call x1, Pallas kernels: 81.5 us -> 76 us  [back(): pl.pallas_call(functools.partial(back_kernel, dp_size, ring, (len(in_spec...]
where the time goes in v2:
time: 185 us; the launch traced here: 183 us
  Pallas kernels  181 us (98%)
    pallas_call x1, Pallas kernels, back(): pl.pallas_call(functools.partial(back_kernel, dp_size, ring, (len(in_spec...  76 us
    pallas_call x1, Pallas kernels, middle(): pl.pallas_call(functools.partial(middle_kernel, dp_size, ring, len(export...  61.9 us
    pallas_call x1, Pallas kernels, front(): pl.pallas_call(functools.partial(front_kernel, dp_size), grid=(2 * half,)...  30.7 us
    pallas_call x1, Pallas kernels, collect(): pl.pallas_call(functools.partial(collect_kernel, 3), grid=(blocks,), in_s...  12.8 us

profile of v2, /device:TPU:0, one launch (start us, length us, event | category | flops | bytes accessed | tf_op | source)
XLA Modules:
  0.0 183.3 jit_solution(16756821926156071616)
XLA Ops:
  0.6 30.7 %front.1 = (bf16[1024,768]{1,0:T(8,128)(2,1)}, bf16[1024,768]{1,0:T(8,128)(2,1)}, bf16[1024,768]{1,0:T(8,128)(2,1)}, bf16[1024,768]{1,0:T(8,128)(2,1)}, bf16[102...) custom-call(bf16[2048,768]{1,0:T(8,128)(2,1)} %refs_0_.3, ...), custom_call_target="tpu_custom_call" | custom-call | tf_op jit(solution)/shard_map/front/pallas_call | solution.py:497
  32.0 61.9 %middle.1 = (f32[2048,768]{1,0:T(8,128)}, f32[1024,768]{1,0:T(8,128)}, bf16[1024,768]{1,0:T(8,128)(2,1)}, f32[2,2,2,2,48,384]{5,4,3,2,1,0:T(8,128)}, f32[2,2,2,2...) custom-call(bf16[2048,768]{1,0:T(8,128)(2,1)} %refs_0_.3, ...), custom_call_target="tpu_custom_call" | custom-call | tf_op jit(solution)/shard_map/middle/pallas_call | solution.py:847
  93.9 76.0 %back.1 = (f32[2048,768]{1,0:T(8,128)}, f32[192,2048]{1,0:T(8,128)}, f32[48,1536]{1,0:T(8,128)}, f32[48,1536]{1,0:T(8,128)}, f32[48,384]{1,0:T(8,128)}, /*index=...) custom-call(bf16[2048,768]{1,0:T(8,128)(2,1)} %refs_0_.3, ...), custom_call_target="tpu_custom_call" | custom-call | tf_op jit(solution)/shard_map/back/pallas_call | solution.py:1383
  169.9 0.0 copy-start
  169.9 12.8 %collect.1 = (f32[2048,768]{1,0:T(8,128)}, f32[2048,768]{1,0:T(8,128)}, f32[192,2048]{1,0:T(8,128)}, f32[48,1536]{1,0:T(8,128)}, f32[48,1536]{1,0:T(8,128)}, /*i...) custom-call(f32[2048,768]{1,0:T(8,128)} %get-tuple-element.55.refs_0_, ...), custom_call_target="tpu_custom_call" | custom-call | tf_op jit(solution)/shard_map/collect/pallas_call | solution.py:1437
  182.7 0.0 copy-done
  182.7 0.5 slice_bitcast_fusion
Async XLA Ops:
  169.9 12.8 %copy-start = (f32[8,128]{1,0:T(8,128)S(1)}, f32[8,128]{1,0:T(8,128)}, u32[]{:S(2)}) copy-start(f32[8,128]{1,0:T(8,128)} %get-tuple-element.82) | copy-start | bytes 12292

commit v3 on v2

--- a/solution.py
+++ b/solution.py
@@ -1428,7 +1428,7 @@
 
 
 def collect(tall, columns, small):
-    blocks = 8
+    blocks = 2
     rows = tall[0]
     specs = [pl.BlockSpec((rows.shape[0] // blocks, rows.shape[1]), lambda i: (i, 0))] * 2 + [
         pl.BlockSpec((columns.shape[0], columns.shape[1] // blocks), lambda i: (0, i)),

time: 185 us -> 182 us (0.984)
  Pallas kernels: 181 us -> 179 us
    pallas_call x1, Pallas kernels: 12.8 us -> 9.93 us  [collect(): pl.pallas_call(functools.partial(collect_kernel, 3), grid=(blocks,), in_s...]
where the time goes in v3:
time: 182 us; the launch traced here: 180 us
  Pallas kernels  179 us (98%)
    pallas_call x1, Pallas kernels, back(): pl.pallas_call(functools.partial(back_kernel, dp_size, ring, (len(in_spec...  76 us
    pallas_call x1, Pallas kernels, middle(): pl.pallas_call(functools.partial(middle_kernel, dp_size, ring, len(export...  61.9 us
    pallas_call x1, Pallas kernels, front(): pl.pallas_call(functools.partial(front_kernel, dp_size), grid=(2 * half,)...  30.7 us
    pallas_call x1, Pallas kernels, collect(): pl.pallas_call(functools.partial(collect_kernel, 3), grid=(blocks,), in_s...  9.93 us

profile of v3, /device:TPU:0, one launch (start us, length us, event | category | flops | bytes accessed | tf_op | source)
XLA Modules:
  0.0 180.4 jit_solution(8627292547883789322)
XLA Ops:
  0.6 30.7 %front.1 = (bf16[1024,768]{1,0:T(8,128)(2,1)}, bf16[1024,768]{1,0:T(8,128)(2,1)}, bf16[1024,768]{1,0:T(8,128)(2,1)}, bf16[1024,768]{1,0:T(8,128)(2,1)}, bf16[102...) custom-call(bf16[2048,768]{1,0:T(8,128)(2,1)} %refs_0_.3, ...), custom_call_target="tpu_custom_call" | custom-call | tf_op jit(solution)/shard_map/front/pallas_call | solution.py:497
  32.0 61.9 %middle.1 = (f32[2048,768]{1,0:T(8,128)}, f32[1024,768]{1,0:T(8,128)}, bf16[1024,768]{1,0:T(8,128)(2,1)}, f32[2,2,2,2,48,384]{5,4,3,2,1,0:T(8,128)}, f32[2,2,2,2...) custom-call(bf16[2048,768]{1,0:T(8,128)(2,1)} %refs_0_.3, ...), custom_call_target="tpu_custom_call" | custom-call | tf_op jit(solution)/shard_map/middle/pallas_call | solution.py:847
  93.9 76.0 %back.1 = (f32[2048,768]{1,0:T(8,128)}, f32[192,2048]{1,0:T(8,128)}, f32[48,1536]{1,0:T(8,128)}, f32[48,1536]{1,0:T(8,128)}, f32[48,384]{1,0:T(8,128)}, /*index=...) custom-call(bf16[2048,768]{1,0:T(8,128)(2,1)} %refs_0_.3, ...), custom_call_target="tpu_custom_call" | custom-call | tf_op jit(solution)/shard_map/back/pallas_call | solution.py:1383
  169.9 0.0 copy-start
  169.9 9.9 %collect.1 = (f32[2048,768]{1,0:T(8,128)}, f32[2048,768]{1,0:T(8,128)}, f32[192,2048]{1,0:T(8,128)}, f32[48,1536]{1,0:T(8,128)}, f32[48,1536]{1,0:T(8,128)}, /*i...) custom-call(f32[2048,768]{1,0:T(8,128)} %get-tuple-element.55.refs_0_, ...), custom_call_target="tpu_custom_call" | custom-call | tf_op jit(solution)/shard_map/collect/pallas_call | solution.py:1437
  179.9 0.0 copy-done
  179.9 0.5 slice_bitcast_fusion
Async XLA Ops:
  169.9 9.9 %copy-start = (f32[8,128]{1,0:T(8,128)S(1)}, f32[8,128]{1,0:T(8,128)}, u32[]{:S(2)}) copy-start(f32[8,128]{1,0:T(8,128)} %get-tuple-element.82) | copy-start | bytes 12292

commit v4 on v3

--- a/solution.py
+++ b/solution.py
@@ -49,7 +49,7 @@
     return pl.ds(pl.multiple_of(index * BLOCK, BLOCK), BLOCK)
 
 
-def recast(source, target, rows=64):
+def recast(source, target, rows=128):
     def one(index):
         part = pl.ds(pl.multiple_of(index * rows, rows), rows)
         target[part, :] = source[part, :].astype(target.dtype)

time: 182 us -> 181 us (level)
  no operation moved by 1% of the time
where the time goes in v4:
time: 181 us; the launch traced here: 180 us
  Pallas kernels  178 us (98%)
    pallas_call x1, Pallas kernels, back(): pl.pallas_call(functools.partial(back_kernel, dp_size, ring, (len(in_spec...  76 us
    pallas_call x1, Pallas kernels, middle(): pl.pallas_call(functools.partial(middle_kernel, dp_size, ring, len(export...  61.9 us
    pallas_call x1, Pallas kernels, front(): pl.pallas_call(functools.partial(front_kernel, dp_size), grid=(2 * half,)...  30.5 us
    pallas_call x1, Pallas kernels, collect(): pl.pallas_call(functools.partial(collect_kernel, 3), grid=(blocks,), in_s...  9.93 us

profile of v4, /device:TPU:0, one launch (start us, length us, event | category | flops | bytes accessed | tf_op | source)
XLA Modules:
  0.0 180.3 jit_solution(3384416324722302857)
XLA Ops:
  0.6 30.5 %front.1 = (bf16[1024,768]{1,0:T(8,128)(2,1)}, bf16[1024,768]{1,0:T(8,128)(2,1)}, bf16[1024,768]{1,0:T(8,128)(2,1)}, bf16[1024,768]{1,0:T(8,128)(2,1)}, bf16[102...) custom-call(bf16[2048,768]{1,0:T(8,128)(2,1)} %refs_0_.3, ...), custom_call_target="tpu_custom_call" | custom-call | tf_op jit(solution)/shard_map/front/pallas_call | solution.py:497
  31.8 61.9 %middle.1 = (f32[2048,768]{1,0:T(8,128)}, f32[1024,768]{1,0:T(8,128)}, bf16[1024,768]{1,0:T(8,128)(2,1)}, f32[2,2,2,2,48,384]{5,4,3,2,1,0:T(8,128)}, f32[2,2,2,2...) custom-call(bf16[2048,768]{1,0:T(8,128)(2,1)} %refs_0_.3, ...), custom_call_target="tpu_custom_call" | custom-call | tf_op jit(solution)/shard_map/middle/pallas_call | solution.py:847
  93.8 76.0 %back.1 = (f32[2048,768]{1,0:T(8,128)}, f32[192,2048]{1,0:T(8,128)}, f32[48,1536]{1,0:T(8,128)}, f32[48,1536]{1,0:T(8,128)}, f32[48,384]{1,0:T(8,128)}, /*index=...) custom-call(bf16[2048,768]{1,0:T(8,128)(2,1)} %refs_0_.3, ...), custom_call_target="tpu_custom_call" | custom-call | tf_op jit(solution)/shard_map/back/pallas_call | solution.py:1383
  169.8 0.0 copy-start
  169.8 9.9 %collect.1 = (f32[2048,768]{1,0:T(8,128)}, f32[2048,768]{1,0:T(8,128)}, f32[192,2048]{1,0:T(8,128)}, f32[48,1536]{1,0:T(8,128)}, f32[48,1536]{1,0:T(8,128)}, /*i...) custom-call(f32[2048,768]{1,0:T(8,128)} %get-tuple-element.55.refs_0_, ...), custom_call_target="tpu_custom_call" | custom-call | tf_op jit(solution)/shard_map/collect/pallas_call | solution.py:1437
  179.7 0.0 copy-done
  179.8 0.5 slice_bitcast_fusion
Async XLA Ops:
  169.8 9.9 %copy-start = (f32[8,128]{1,0:T(8,128)S(1)}, f32[8,128]{1,0:T(8,128)}, u32[]{:S(2)}) copy-start(f32[8,128]{1,0:T(8,128)} %get-tuple-element.82) | copy-start | bytes 12292
